TPU v7x, 32 devices: a whole 2x2x4 slice. The times are simulated.
32 devices in a mesh: mem: 8 (over y, x, core), lat: 4 (over z).
Axes of the slice: x: 2, y: 2, z: 4, core: 2. Of those that a mesh axis runs over, the one named last changes fastest.
Arguments:
- coarse_weights: bfloat16 [32, 32, 8, 128], P('lat', 'mem'), may hold values from -6 to 6
- perturbations: bfloat16 [32, 8, 128, 512], P('mem', None, 'lat'), may hold values from -6 to 6
- lat_matrix: bfloat16 [128, 32], P('lat'), may hold values from -1 to 1
- lon_matrix: bfloat16 [128, 512], replicated, may hold values from -0.5 to 0.5
- wind_field: float32 [2, 128, 512], P(None, 'lat', 'mem'), may hold values from -0.4 to 0.4
- observed_cell: int32 [4, 8, 128, 64], P(None, None, 'lat', 'mem'), may hold values from 0 to 7
- observed_value: float32 [4, 8, 128, 64], P(None, None, 'lat', 'mem'), may hold values from -6 to 6
- observed_weight: float32 [4, 8, 128, 64], P(None, None, 'lat', 'mem'), may hold values from 0.5 to 4
Outputs:
- gradient: float32 [32, 32, 8, 128], P('lat', 'mem')
- increment: float32 [8, 128, 512], P(None, 'lat', 'mem')
Inputs may be any that keep to these rules, and one draw needn't show every extreme that they name: `observed_cell`: the observed cell is an offset within its block of 8 longitudes.
All inputs are finite; a program needn't handle non-finite values.
Results may differ from a plain program's by a relative error of at most 0.0003.
Values may be sent and summed in bfloat16 or wider, within the bound.
A program may use at most 64 MiB of HBM per device.

v0:
```python
import jax
import jax.numpy as jnp
from jax import lax
from jax.sharding import PartitionSpec as P

STEPS = 4
OBLK = 8


diffusion = 0.2
highest = lax.Precision.HIGHEST


def padded_2(value, sides, width):
    for axis, dim in sides:
        peers, length = (lax.axis_size(axis), value.shape[dim])
        up = [(i, (i + 1) % peers) for i in range(peers - 1)]
        down = [(j, i) for i, j in up]
        last = lax.slice_in_dim(value, length - width, length, axis=dim)
        initial = lax.slice_in_dim(value, 0, width, axis=dim)
        before = lax.ppermute(last, axis, up)
        after = lax.ppermute(initial, axis, down)
        value = jnp.concatenate([before, value, after], axis=dim)
    return value


def stencil_parts(padded):
    center = padded[:, 1:-1, 1:-1]
    north_cell = padded[:, 2:, 1:-1]
    south_cell = padded[:, :-2, 1:-1]
    east_cell = padded[:, 1:-1, 2:]
    west_cell = padded[:, 1:-1, :-2]
    return (center, north_cell, south_cell, east_cell, west_cell)


def advance(padded, wind_out):
    center, north_cell, south_cell, east_cell, west_cell = stencil_parts(padded)
    spread = north_cell + south_cell + east_cell + west_cell - 4.0 * center
    return (
        center
        + diffusion * spread
        - 0.5 * wind_out[1] * (north_cell - south_cell)
        - 0.5 * wind_out[0] * (east_cell - west_cell)
    )


def retreat(padded, wind_in):
    center, north_cell, south_cell, east_cell, west_cell = stencil_parts(padded)
    spread = north_cell + south_cell + east_cell + west_cell - 4.0 * center
    along_lon = wind_in[0] * padded
    along_lat = wind_in[1] * padded
    return (
        center
        + diffusion * spread
        + 0.5 * (along_lat[:, 2:, 1:-1] - along_lat[:, :-2, 1:-1])
        + 0.5 * (along_lon[:, 1:-1, 2:] - along_lon[:, 1:-1, :-2])
    )


def observe(tangent, picked, observed, weighting):
    levels, row_count, col_count = tangent.shape
    blocks = tangent.reshape(levels, row_count, col_count // OBLK, OBLK)
    onehot = (picked[..., None] == jnp.arange(OBLK, dtype=jnp.int32)).astype(jnp.float32)
    looked = jnp.sum(blocks * onehot, axis=-1)
    misfit = weighting * (looked - observed)
    return (misfit[..., None] * onehot).reshape(levels, row_count, col_count)


def domain_mask(margin, row_count, col_count):
    lat_start = lax.axis_index("lat") * row_count - margin
    lon_start = lax.axis_index("mem") * col_count - margin
    row_place = lat_start + jnp.arange(row_count + 2 * margin, dtype=jnp.int32)
    col_place = lon_start + jnp.arange(col_count + 2 * margin, dtype=jnp.int32)
    rows_inside = (row_place >= 0) & (row_place < row_count * lax.axis_size("lat"))
    cols_inside = (col_place >= 0) & (col_place < col_count * lax.axis_size("mem"))
    return (rows_inside[:, None] & cols_inside[None, :]).astype(jnp.float32)


def body(
    coarse_weights,
    perturbations,
    lat_matrix,
    lon_matrix,
    wind_field,
    observed_cell,
    observed_value,
    observed_weight,
):
    members_here, levels, row_count, lon_total = perturbations.shape
    col_count = wind_field.shape[2]
    members_all = members_here * lax.axis_size("mem")
    member_scale = 1.0 / jnp.sqrt(jnp.float32(members_all - 1))
    lat_full = lat_matrix.astype(jnp.float32)
    lon_full = lon_matrix.astype(jnp.float32)
    widened = jnp.einsum(
        "cmlw,wf->cmlf", coarse_weights.astype(jnp.float32), lon_full, precision=highest
    )
    columns = lat_full
    localized = jnp.einsum(
        "rc,cmlf->mlrf",
        columns,
        lax.all_gather(widened, "lat", axis=0, tiled=True),
        precision=highest,
    )
    partial_sum = jnp.sum(localized * perturbations, axis=0)
    increment = lax.psum_scatter(partial_sum, "mem", scatter_dimension=2, tiled=True) * member_scale
    wide_wind = padded_2(wind_field, (("mem", 2), ("lat", 1)), STEPS)

    def wind_margin(margin):
        return wide_wind[
            :,
            STEPS - margin : STEPS + row_count + margin,
            STEPS - margin : STEPS + col_count + margin,
        ]

    forcings = []
    tangent = padded_2(increment, (("mem", 2), ("lat", 1)), STEPS)
    for step_index in range(STEPS):
        margin = STEPS - step_index - 1
        tangent = advance(tangent, wind_margin(margin)) * domain_mask(margin, row_count, col_count)
        inner = tangent[:, margin : margin + row_count, margin : margin + col_count]
        forcings.append(
            observe(
                inner,
                observed_cell[step_index],
                observed_value[step_index],
                observed_weight[step_index],
            )
        )
    adjoint = jnp.zeros_like(increment)
    for step_index in reversed(range(STEPS)):
        padded = padded_2(adjoint + forcings[step_index], (("mem", 2), ("lat", 1)), 1)
        adjoint = retreat(padded, wind_margin(1))
    product = perturbations * lax.all_gather(adjoint, "mem", axis=2, tiled=True)[None]
    projected = jnp.einsum("mlrf,wf->mlrw", product, lon_full, precision=highest)
    columns = lat_full
    banded = lax.psum_scatter(
        jnp.einsum("rc,mlrw->cmlw", columns, projected, precision=highest),
        "lat",
        scatter_dimension=0,
        tiled=True,
    )
    gradient = banded * member_scale + coarse_weights.astype(jnp.float32)
    return (gradient, increment)


def solution(mesh):
    in_specs = (
        P("lat", "mem", None, None),
        P("mem", None, "lat", None),
        P("lat", None),
        P(),
        P(None, "lat", "mem"),
        P(None, None, "lat", "mem"),
        P(None, None, "lat", "mem"),
        P(None, None, "lat", "mem"),
    )
    out_specs = (P("lat", "mem", None, None), P(None, "lat", "mem"))
    return jax.shard_map(body, mesh=mesh, in_specs=in_specs, out_specs=out_specs, check_vma=False)
```

profile of v0, /device:TPU:0, one launch (start us, length us, event | category | flops | bytes accessed | tf_op | source)
XLA Modules:
  0.0 257.9 jit_solution(16076721269377844049)
XLA Ops:
  7.2 0.8 copy-done
  8.1 1.9 fusion.53
  10.0 1.5 fusion.76
  11.5 2.4 collective-permute-start.4
  13.9 1.3 collective-permute-start.5
  15.4 0.7 and_convert_fusion.2
  16.0 0.7 and_convert_fusion.1
  16.7 0.7 and_convert_fusion
  17.4 0.7 multiply_bitcast_fusion.3
  18.2 0.8 slice_bitcast_fusion.2
  19.0 39.5 %all-gather.2.cloned.1.call-done = f32[32,4,8,512]{3,0,2,1:T(8,128)} async-done(((f32[8,4,8,512]{3,0,2,1:T(8,128)}), f32[32,4,8,512]{3,0,2,1:T(8,128)}) %all-gather.2.cloned.1.call-update) | async-done | bytes 2097168 | tf_op jit(solution)/shard_map/all_gather | solution.py:102
  58.5 3.7 %fusion = f32[8,32,512]{2,1,0:T(8,128)} fusion(bf16[4,8,32,512]{3,2,1,0:T(8,128)(2,1)S(1)} %copy-done.1, f32[32,4,8,512]{3,0,2,1:T(8,128)} %all-gather.2.cloned.1.call-done, bf16[32,32]{1,0:T(8,128)(2,1)} %param.10), kind=kOutput, calls=%fused_computation.2 | convolution fusion | flops 202768384 | bytes 3672064 | tf_op jit(solution)/shard_map/rc,cmlf->mlrf/dot_general | solution.py:99
  62.2 1.8 copy.254
  64.1 1.4 reshape.260
  65.7 2.1 collective-permute-start.6
  67.8 1.3 collective-permute-start.7
  69.4 3.9 %collective-permute-done.7 = f32[2,4,72]{2,1,0:T(4,128)S(1)} collective-permute-done((f32[2,4,72]{2,1,0:T(4,128)S(1)}, f32[2,4,72]{2,1,0:T(4,128)S(1)}, u32[]{:S(2)}, u32[]{:S(2)}) %collective-permute-start.7) | collective-permute-done | bytes 2336 | tf_op jit(solution)/shard_map/ppermute | solution.py:22
  73.3 0.9 pad_maximum_fusion.42
  74.2 24.3 %reduce-scatter.7.cloned.1.call-done = f32[64,256]{1,0:T(8,128)} async-done(((f32[512,256]{1,0:T(8,128)}), f32[64,256]{1,0:T(8,128)}) %reduce-scatter.7.cloned.1.call-update) | async-done | bytes 65552
  98.5 0.9 reshape.261
  99.8 1.3 collective-permute-start
  101.1 1.3 collective-permute-start.1
  102.5 3.5 %collective-permute-done.1 = f32[8,32,4]{2,1,0:T(8,128)S(1)} collective-permute-done((f32[8,32,4]{2,1,0:T(8,128)S(1)}, f32[8,32,4]{2,1,0:T(8,128)S(1)}, u32[]{:S(2)}, u32[]{:S(2)}) %collective-permute-start.1) | collective-permute-done | bytes 4128 | tf_op jit(solution)/shard_map/ppermute | solution.py:22
  106.3 3.4 %collective-permute-start.2 = (f32[8,4,72]{1,2,0:T(8,128)S(1)}, f32[8,4,72]{1,2,0:T(8,128)S(1)}, u32[]{:S(2)}, u32[]{:S(2)}) collective-permute-start(f32[8,4,72]{1,2,0:T(8,128)S(1)} %copy.233), channel_id=1, source_target_pairs={{0,1},{1,2},{2,3},{4,5},{5,6},{6,7},{8,9},{9,10},{10,11},{12,13},{... | collective-permute-start | bytes 27656 | tf_op jit(solution)/shard_map/ppermute | solution.py:21
  109.9 1.3 collective-permute-start.3
  112.1 2.5 collective-permute-done.2
  114.6 4.9 %collective-permute-done.3 = f32[8,4,72]{1,2,0:T(8,128)S(1)} collective-permute-done((f32[8,4,72]{1,2,0:T(8,128)S(1)}, f32[8,4,72]{1,2,0:T(8,128)S(1)}, u32[]{:S(2)}, u32[]{:S(2)}) %collective-permute-start.3) | collective-permute-done | bytes 9248 | tf_op jit(solution)/shard_map/ppermute | solution.py:22
  121.7 4.0 %collective-permute-start.8 = (f32[8,32,1]{1,2,0:T(1,128)S(1)}, f32[8,32,1]{1,2,0:T(1,128)S(1)}, u32[]{:S(2)}, u32[]{:S(2)}) collective-permute-start(f32[8,32,1]{1,2,0:T(1,128)S(1)} %get-tuple-element.40), channel_id=1, source_target_pairs={{0,4},{4,8},{8,12},{12,16},{16,20},{20,24},{24,28},{1,5},{5,9},{9,... | collective-permute-start | bytes 3080 | tf_op jit(solution)/shard_map/ppermute | solution.py:21
  125.8 1.3 collective-permute-start.9
  127.1 3.5 %collective-permute-done.9 = f32[8,32,1]{1,2,0:T(1,128)S(1)} collective-permute-done((f32[8,32,1]{1,2,0:T(1,128)S(1)}, f32[8,32,1]{1,2,0:T(1,128)S(1)}, u32[]{:S(2)}, u32[]{:S(2)}) %collective-permute-start.9) | collective-permute-done | bytes 1056 | tf_op jit(solution)/shard_map/ppermute | solution.py:22
  130.8 1.3 collective-permute-start.10
  132.1 4.6 %collective-permute-start.11 = (f32[8,1,66]{1,2,0:T(8,128)S(1)}, f32[8,1,66]{1,2,0:T(8,128)S(1)}, u32[]{:S(2)}, u32[]{:S(2)}) collective-permute-start(f32[8,1,66]{1,2,0:T(8,128)S(1)} %get-tuple-element.28), channel_id=1, source_target_pairs={{0,1},{1,2},{2,3},{4,5},{5,6},{6,7},{8,9},{9,10},{10,11},{12,13},{... | collective-permute-start | bytes 6344 | tf_op jit(solution)/shard_map/ppermute | solution.py:21
  136.8 4.3 %collective-permute-done.10 = f32[8,1,66]{1,2,0:T(8,128)S(1)} collective-permute-done((f32[8,1,66]{1,2,0:T(8,128)S(1)}, f32[8,1,66]{1,2,0:T(8,128)S(1)}, u32[]{:S(2)}, u32[]{:S(2)}) %collective-permute-start.10) | collective-permute-done | bytes 2144 | tf_op jit(solution)/shard_map/ppermute | solution.py:22
  141.1 1.7 collective-permute-done.11
  143.1 0.5 fusion.41
  143.7 3.1 %collective-permute-start.12 = (f32[8,32,1]{1,2,0:T(1,128)S(1)}, f32[8,32,1]{1,2,0:T(1,128)S(1)}, u32[]{:S(2)}, u32[]{:S(2)}) collective-permute-start(f32[8,32,1]{1,2,0:T(1,128)S(1)} %get-tuple-element.38), channel_id=1, source_target_pairs={{0,4},{4,8},{8,12},{12,16},{16,20},{20,24},{24,28},{1,5},{5,9},{9,... | collective-permute-start | bytes 3080 | tf_op jit(solution)/shard_map/ppermute | solution.py:21
  146.8 1.3 collective-permute-start.13
  148.1 1.8 collective-permute-done.13
  150.1 1.3 collective-permute-start.14
  151.4 4.9 %collective-permute-start.15 = (f32[8,1,66]{1,2,0:T(8,128)S(1)}, f32[8,1,66]{1,2,0:T(8,128)S(1)}, u32[]{:S(2)}, u32[]{:S(2)}) collective-permute-start(f32[8,1,66]{1,2,0:T(8,128)S(1)} %get-tuple-element.26), channel_id=1, source_target_pairs={{0,1},{1,2},{2,3},{4,5},{5,6},{6,7},{8,9},{9,10},{10,11},{12,13},{... | collective-permute-start | bytes 6344 | tf_op jit(solution)/shard_map/ppermute | solution.py:21
  156.3 4.1 %collective-permute-done.14 = f32[8,1,66]{1,2,0:T(8,128)S(1)} collective-permute-done((f32[8,1,66]{1,2,0:T(8,128)S(1)}, f32[8,1,66]{1,2,0:T(8,128)S(1)}, u32[]{:S(2)}, u32[]{:S(2)}) %collective-permute-start.14) | collective-permute-done | bytes 2144 | tf_op jit(solution)/shard_map/ppermute | solution.py:22
  160.4 1.7 collective-permute-done.15
  162.4 0.5 fusion.30
  162.9 3.5 %collective-permute-start.16 = (f32[8,32,1]{1,2,0:T(1,128)S(1)}, f32[8,32,1]{1,2,0:T(1,128)S(1)}, u32[]{:S(2)}, u32[]{:S(2)}) collective-permute-start(f32[8,32,1]{1,2,0:T(1,128)S(1)} %get-tuple-element.36), channel_id=1, source_target_pairs={{0,4},{4,8},{8,12},{12,16},{16,20},{20,24},{24,28},{1,5},{5,9},{9,... | collective-permute-start | bytes 3080 | tf_op jit(solution)/shard_map/ppermute | solution.py:21
  166.5 1.3 collective-permute-start.17
  167.8 1.8 collective-permute-done.17
  169.7 1.3 collective-permute-start.18
  171.0 5.0 %collective-permute-start.19 = (f32[8,1,66]{1,2,0:T(8,128)S(1)}, f32[8,1,66]{1,2,0:T(8,128)S(1)}, u32[]{:S(2)}, u32[]{:S(2)}) collective-permute-start(f32[8,1,66]{1,2,0:T(8,128)S(1)} %get-tuple-element.24), channel_id=1, source_target_pairs={{0,1},{1,2},{2,3},{4,5},{5,6},{6,7},{8,9},{9,10},{10,11},{12,13},{... | collective-permute-start | bytes 6344 | tf_op jit(solution)/shard_map/ppermute | solution.py:21
  176.0 4.2 %collective-permute-done.18 = f32[8,1,66]{1,2,0:T(8,128)S(1)} collective-permute-done((f32[8,1,66]{1,2,0:T(8,128)S(1)}, f32[8,1,66]{1,2,0:T(8,128)S(1)}, u32[]{:S(2)}, u32[]{:S(2)}) %collective-permute-start.18) | collective-permute-done | bytes 2144 | tf_op jit(solution)/shard_map/ppermute | solution.py:22
  180.2 1.7 collective-permute-done.19
  182.7 3.5 %collective-permute-start.20 = (f32[8,32,1]{1,2,0:T(1,128)S(1)}, f32[8,32,1]{1,2,0:T(1,128)S(1)}, u32[]{:S(2)}, u32[]{:S(2)}) collective-permute-start(f32[8,32,1]{1,2,0:T(1,128)S(1)} %get-tuple-element.30), channel_id=1, source_target_pairs={{0,4},{4,8},{8,12},{12,16},{16,20},{20,24},{24,28},{1,5},{5,9},{9,... | collective-permute-start | bytes 3080 | tf_op jit(solution)/shard_map/ppermute | solution.py:21
  186.2 1.3 collective-permute-start.21
  187.5 2.0 collective-permute-done.21
  189.6 1.3 collective-permute-start.22
  190.9 5.0 %collective-permute-start.23 = (f32[8,1,66]{1,2,0:T(8,128)S(1)}, f32[8,1,66]{1,2,0:T(8,128)S(1)}, u32[]{:S(2)}, u32[]{:S(2)}) collective-permute-start(f32[8,1,66]{1,2,0:T(8,128)S(1)} %get-tuple-element.22), channel_id=1, source_target_pairs={{0,1},{1,2},{2,3},{4,5},{5,6},{6,7},{8,9},{9,10},{10,11},{12,13},{... | collective-permute-start | bytes 6344 | tf_op jit(solution)/shard_map/ppermute | solution.py:21
  196.0 4.2 %collective-permute-done.22 = f32[8,1,66]{1,2,0:T(8,128)S(1)} collective-permute-done((f32[8,1,66]{1,2,0:T(8,128)S(1)}, f32[8,1,66]{1,2,0:T(8,128)S(1)}, u32[]{:S(2)}, u32[]{:S(2)}) %collective-permute-start.22) | collective-permute-done | bytes 2144 | tf_op jit(solution)/shard_map/ppermute | solution.py:22
  200.2 1.7 collective-permute-done.23
  202.7 17.4 %all_gather.7 = f32[8,32,512]{1,2,0:T(8,128)S(1)} all-gather(f32[8,32,64]{1,2,0:T(8,128)S(1)} %fusion.4), channel_id=1, replica_groups=mesh['mem'=8,'lat'=4] {'mem'}, dimensions={2}, use_global_device_ids=true | all-gather | bytes 589824 | tf_op jit(solution)/shard_map/all_gather | solution.py:134
  220.1 1.4 copy.246
  221.5 2.2 fusion.1
  223.8 1.2 convolution_bitcast_fusion
  225.0 24.8 %reduce-scatter.5.cloned.1.call-done = f32[8,4,8,128]{3,0,2,1:T(8,128)} async-done(((f32[32,4,8,128]{3,0,2,1:T(8,128)}), f32[8,4,8,128]{3,0,2,1:T(8,128)}) %reduce-scatter.5.cloned.1.call-update) | async-done | bytes 131088 | tf_op jit(solution)/shard_map/reduce_scatter | solution.py:137
  249.8 0.9 convert_add_fusion
  250.7 0.7 copy.249
  (98 shorter events, 7.5 us)
Async XLA Ops:
  7.2 0.9 copy-start
  7.2 51.3 %copy-start.1 = (bf16[4,8,32,512]{3,2,1,0:T(8,128)(2,1)S(1)}, bf16[4,8,32,512]{3,2,1,0:T(8,128)(2,1)}, u32[]{:S(2)}) copy-start(bf16[4,8,32,512]{3,2,1,0:T(8,128)(2,1)} %param.9) | copy-start | bytes 3145732
  7.2 51.3 %all-gather.2.cloned.1.call-start = ((), (), s32[]{:S(2)}) async-start(), calls=%async_computation.2 | async-start | bytes 2621440 | tf_op jit(solution)/shard_map/all_gather | solution.py:102
  10.0 88.6 %reduce-scatter.7.cloned.1.call-start = ((), (), s32[]{:S(2)}) async-start(), calls=%async_computation.4 | async-start | bytes 589824
  11.5 54.0 %collective-permute-start.4 = (f32[2,32,4]{2,1,0:T(8,128)}, f32[2,32,4]{2,1,0:T(8,128)S(1)}, u32[]{:S(2)}, u32[]{:S(2)}) collective-permute-start(f32[2,32,4]{2,1,0:T(8,128)} %get-tuple-element.62), channel_id=1, source_target_pairs={{0,4},{4,8},{8,12},{12,16},{16,20},{20,24},{24,28},{1,5},{5,9},{9,... | collective-permute-start | bytes 3080 | tf_op jit(solution)/shard_map/ppermute | solution.py:21
  13.9 51.6 %collective-permute-start.5 = (f32[2,32,4]{2,1,0:T(8,128)}, f32[2,32,4]{2,1,0:T(8,128)S(1)}, u32[]{:S(2)}, u32[]{:S(2)}) collective-permute-start(f32[2,32,4]{2,1,0:T(8,128)} %get-tuple-element.63), channel_id=1, source_target_pairs={{4,0},{8,4},{12,8},{16,12},{20,16},{24,20},{28,24},{5,1},{9,5},{13... | collective-permute-start | bytes 3080 | tf_op jit(solution)/shard_map/ppermute | solution.py:22
  64.1 1.5 copy-start.3
  65.5 184.3 %reduce-scatter.5.cloned.1.call-start = ((), (), s32[]{:S(2)}) async-start(), calls=%async_computation.3 | async-start | bytes 655360 | tf_op jit(solution)/shard_map/reduce_scatter | solution.py:137
  65.6 2.2 copy-start.8
  65.6 3.6 %copy-start.9 = (f32[2,32,4]{2,1,0:T(8,128)}, f32[2,32,4]{2,1,0:T(8,128)S(1)}, u32[]{:S(2)}) copy-start(f32[2,32,4]{2,1,0:T(8,128)S(1)} %collective-permute-done.5) | copy-start | bytes 3076
  65.7 3.7 %collective-permute-start.6 = (f32[2,4,72]{2,1,0:T(4,128)S(1)}, f32[2,4,72]{2,1,0:T(4,128)S(1)}, u32[]{:S(2)}, u32[]{:S(2)}) collective-permute-start(f32[2,4,72]{2,1,0:T(4,128)S(1)} %get-tuple-element.50), channel_id=1, source_target_pairs={{0,1},{1,2},{2,3},{4,5},{5,6},{6,7},{8,9},{9,10},{10,11},{12,13},{... | collective-permute-start | bytes 6920 | tf_op jit(solution)/shard_map/ppermute | solution.py:21
  67.8 5.5 %collective-permute-start.7 = (f32[2,4,72]{2,1,0:T(4,128)S(1)}, f32[2,4,72]{2,1,0:T(4,128)S(1)}, u32[]{:S(2)}, u32[]{:S(2)}) collective-permute-start(f32[2,4,72]{2,1,0:T(4,128)S(1)} %get-tuple-element.51), channel_id=1, source_target_pairs={{1,0},{2,1},{3,2},{5,4},{6,5},{7,6},{9,8},{10,9},{11,10},{13,12},{... | collective-permute-start | bytes 6920 | tf_op jit(solution)/shard_map/ppermute | solution.py:22
  99.6 20.0 %copy-start.7 = (f32[38,70]{0,1:T(8,128)S(1)}, f32[38,70]{0,1:T(8,128)}, u32[]{:S(2)}) copy-start(f32[38,70]{0,1:T(8,128)} %and_convert_fusion.2) | copy-start | bytes 31924
  99.7 20.4 %copy-start.2 = (f32[8,32,64]{2,1,0:T(8,128)}, f32[8,32,64]{2,1,0:T(8,128)S(1)}, u32[]{:S(2)}) copy-start(f32[8,32,64]{2,1,0:T(8,128)S(1)} %broadcast_multiply_fusion.8) | copy-start | bytes 196612
  99.8 2.7 %collective-permute-start = (f32[8,32,4]{2,1,0:T(8,128)S(1)}, f32[8,32,4]{2,1,0:T(8,128)S(1)}, u32[]{:S(2)}, u32[]{:S(2)}) collective-permute-start(f32[8,32,4]{2,1,0:T(8,128)S(1)} %get-tuple-element.48), channel_id=1, source_target_pairs={{0,4},{4,8},{8,12},{12,16},{16,20},{20,24},{24,28},{1,5},{5,9},{9,... | collective-permute-start | bytes 12296 | tf_op jit(solution)/shard_map/ppermute | solution.py:21
  101.1 4.9 %collective-permute-start.1 = (f32[8,32,4]{2,1,0:T(8,128)S(1)}, f32[8,32,4]{2,1,0:T(8,128)S(1)}, u32[]{:S(2)}, u32[]{:S(2)}) collective-permute-start(f32[8,32,4]{2,1,0:T(8,128)S(1)} %get-tuple-element.49), channel_id=1, source_target_pairs={{4,0},{8,4},{12,8},{16,12},{20,16},{24,20},{28,24},{5,1},{9,5},{13... | collective-permute-start | bytes 12296 | tf_op jit(solution)/shard_map/ppermute | solution.py:22
  106.3 8.2 %collective-permute-start.2 = (f32[8,4,72]{1,2,0:T(8,128)S(1)}, f32[8,4,72]{1,2,0:T(8,128)S(1)}, u32[]{:S(2)}, u32[]{:S(2)}) collective-permute-start(f32[8,4,72]{1,2,0:T(8,128)S(1)} %copy.233), channel_id=1, source_target_pairs={{0,1},{1,2},{2,3},{4,5},{5,6},{6,7},{8,9},{9,10},{10,11},{12,13},{... | collective-permute-start | bytes 27656 | tf_op jit(solution)/shard_map/ppermute | solution.py:21
  109.8 10.3 %copy-start.6 = (f32[36,68]{0,1:T(8,128)S(1)}, f32[36,68]{0,1:T(8,128)}, u32[]{:S(2)}) copy-start(f32[36,68]{0,1:T(8,128)} %and_convert_fusion.1) | copy-start | bytes 29380
  109.9 9.5 %collective-permute-start.3 = (f32[8,4,72]{1,2,0:T(8,128)S(1)}, f32[8,4,72]{1,2,0:T(8,128)S(1)}, u32[]{:S(2)}, u32[]{:S(2)}) collective-permute-start(f32[8,4,72]{1,2,0:T(8,128)S(1)} %copy.234), channel_id=1, source_target_pairs={{1,0},{2,1},{3,2},{5,4},{6,5},{7,6},{9,8},{10,9},{11,10},{13,12},{... | collective-permute-start | bytes 27656 | tf_op jit(solution)/shard_map/ppermute | solution.py:22
  119.7 1.1 copy-start.5
  120.5 1.1 copy-start.10
  120.5 1.1 copy-start.11
  121.7 5.3 %collective-permute-start.8 = (f32[8,32,1]{1,2,0:T(1,128)S(1)}, f32[8,32,1]{1,2,0:T(1,128)S(1)}, u32[]{:S(2)}, u32[]{:S(2)}) collective-permute-start(f32[8,32,1]{1,2,0:T(1,128)S(1)} %get-tuple-element.40), channel_id=1, source_target_pairs={{0,4},{4,8},{8,12},{12,16},{16,20},{20,24},{24,28},{1,5},{5,9},{9,... | collective-permute-start | bytes 3080 | tf_op jit(solution)/shard_map/ppermute | solution.py:21
  125.8 4.8 %collective-permute-start.9 = (f32[8,32,1]{1,2,0:T(1,128)S(1)}, f32[8,32,1]{1,2,0:T(1,128)S(1)}, u32[]{:S(2)}, u32[]{:S(2)}) collective-permute-start(f32[8,32,1]{1,2,0:T(1,128)S(1)} %get-tuple-element.41), channel_id=1, source_target_pairs={{4,0},{8,4},{12,8},{16,12},{20,16},{24,20},{28,24},{5,1},{9,5},{13... | collective-permute-start | bytes 3080 | tf_op jit(solution)/shard_map/ppermute | solution.py:22
  130.8 10.4 %collective-permute-start.10 = (f32[8,1,66]{1,2,0:T(8,128)S(1)}, f32[8,1,66]{1,2,0:T(8,128)S(1)}, u32[]{:S(2)}, u32[]{:S(2)}) collective-permute-start(f32[8,1,66]{1,2,0:T(8,128)S(1)} %get-tuple-element.29), channel_id=1, source_target_pairs={{1,0},{2,1},{3,2},{5,4},{6,5},{7,6},{9,8},{10,9},{11,10},{13,12},{... | collective-permute-start | bytes 6344 | tf_op jit(solution)/shard_map/ppermute | solution.py:22
  132.1 10.8 %collective-permute-start.11 = (f32[8,1,66]{1,2,0:T(8,128)S(1)}, f32[8,1,66]{1,2,0:T(8,128)S(1)}, u32[]{:S(2)}, u32[]{:S(2)}) collective-permute-start(f32[8,1,66]{1,2,0:T(8,128)S(1)} %get-tuple-element.28), channel_id=1, source_target_pairs={{0,1},{1,2},{2,3},{4,5},{5,6},{6,7},{8,9},{9,10},{10,11},{12,13},{... | collective-permute-start | bytes 6344 | tf_op jit(solution)/shard_map/ppermute | solution.py:21
  143.7 4.5 %collective-permute-start.12 = (f32[8,32,1]{1,2,0:T(1,128)S(1)}, f32[8,32,1]{1,2,0:T(1,128)S(1)}, u32[]{:S(2)}, u32[]{:S(2)}) collective-permute-start(f32[8,32,1]{1,2,0:T(1,128)S(1)} %get-tuple-element.38), channel_id=1, source_target_pairs={{0,4},{4,8},{8,12},{12,16},{16,20},{20,24},{24,28},{1,5},{5,9},{9,... | collective-permute-start | bytes 3080 | tf_op jit(solution)/shard_map/ppermute | solution.py:21
  146.8 3.1 %collective-permute-start.13 = (f32[8,32,1]{1,2,0:T(1,128)S(1)}, f32[8,32,1]{1,2,0:T(1,128)S(1)}, u32[]{:S(2)}, u32[]{:S(2)}) collective-permute-start(f32[8,32,1]{1,2,0:T(1,128)S(1)} %get-tuple-element.39), channel_id=1, source_target_pairs={{4,0},{8,4},{12,8},{16,12},{20,16},{24,20},{28,24},{5,1},{9,5},{13... | collective-permute-start | bytes 3080 | tf_op jit(solution)/shard_map/ppermute | solution.py:22
  150.1 10.3 %collective-permute-start.14 = (f32[8,1,66]{1,2,0:T(8,128)S(1)}, f32[8,1,66]{1,2,0:T(8,128)S(1)}, u32[]{:S(2)}, u32[]{:S(2)}) collective-permute-start(f32[8,1,66]{1,2,0:T(8,128)S(1)} %get-tuple-element.27), channel_id=1, source_target_pairs={{1,0},{2,1},{3,2},{5,4},{6,5},{7,6},{9,8},{10,9},{11,10},{13,12},{... | collective-permute-start | bytes 6344 | tf_op jit(solution)/shard_map/ppermute | solution.py:22
  151.4 10.8 %collective-permute-start.15 = (f32[8,1,66]{1,2,0:T(8,128)S(1)}, f32[8,1,66]{1,2,0:T(8,128)S(1)}, u32[]{:S(2)}, u32[]{:S(2)}) collective-permute-start(f32[8,1,66]{1,2,0:T(8,128)S(1)} %get-tuple-element.26), channel_id=1, source_target_pairs={{0,1},{1,2},{2,3},{4,5},{5,6},{6,7},{8,9},{9,10},{10,11},{12,13},{... | collective-permute-start | bytes 6344 | tf_op jit(solution)/shard_map/ppermute | solution.py:21
  162.9 4.8 %collective-permute-start.16 = (f32[8,32,1]{1,2,0:T(1,128)S(1)}, f32[8,32,1]{1,2,0:T(1,128)S(1)}, u32[]{:S(2)}, u32[]{:S(2)}) collective-permute-start(f32[8,32,1]{1,2,0:T(1,128)S(1)} %get-tuple-element.36), channel_id=1, source_target_pairs={{0,4},{4,8},{8,12},{12,16},{16,20},{20,24},{24,28},{1,5},{5,9},{9,... | collective-permute-start | bytes 3080 | tf_op jit(solution)/shard_map/ppermute | solution.py:21
  166.5 3.1 %collective-permute-start.17 = (f32[8,32,1]{1,2,0:T(1,128)S(1)}, f32[8,32,1]{1,2,0:T(1,128)S(1)}, u32[]{:S(2)}, u32[]{:S(2)}) collective-permute-start(f32[8,32,1]{1,2,0:T(1,128)S(1)} %get-tuple-element.37), channel_id=1, source_target_pairs={{4,0},{8,4},{12,8},{16,12},{20,16},{24,20},{28,24},{5,1},{9,5},{13... | collective-permute-start | bytes 3080 | tf_op jit(solution)/shard_map/ppermute | solution.py:22
  169.7 10.4 %collective-permute-start.18 = (f32[8,1,66]{1,2,0:T(8,128)S(1)}, f32[8,1,66]{1,2,0:T(8,128)S(1)}, u32[]{:S(2)}, u32[]{:S(2)}) collective-permute-start(f32[8,1,66]{1,2,0:T(8,128)S(1)} %get-tuple-element.25), channel_id=1, source_target_pairs={{1,0},{2,1},{3,2},{5,4},{6,5},{7,6},{9,8},{10,9},{11,10},{13,12},{... | collective-permute-start | bytes 6344 | tf_op jit(solution)/shard_map/ppermute | solution.py:22
  171.0 10.9 %collective-permute-start.19 = (f32[8,1,66]{1,2,0:T(8,128)S(1)}, f32[8,1,66]{1,2,0:T(8,128)S(1)}, u32[]{:S(2)}, u32[]{:S(2)}) collective-permute-start(f32[8,1,66]{1,2,0:T(8,128)S(1)} %get-tuple-element.24), channel_id=1, source_target_pairs={{0,1},{1,2},{2,3},{4,5},{5,6},{6,7},{8,9},{9,10},{10,11},{12,13},{... | collective-permute-start | bytes 6344 | tf_op jit(solution)/shard_map/ppermute | solution.py:21
  182.7 4.8 %collective-permute-start.20 = (f32[8,32,1]{1,2,0:T(1,128)S(1)}, f32[8,32,1]{1,2,0:T(1,128)S(1)}, u32[]{:S(2)}, u32[]{:S(2)}) collective-permute-start(f32[8,32,1]{1,2,0:T(1,128)S(1)} %get-tuple-element.30), channel_id=1, source_target_pairs={{0,4},{4,8},{8,12},{12,16},{16,20},{20,24},{24,28},{1,5},{5,9},{9,... | collective-permute-start | bytes 3080 | tf_op jit(solution)/shard_map/ppermute | solution.py:21
  186.2 3.3 %collective-permute-start.21 = (f32[8,32,1]{1,2,0:T(1,128)S(1)}, f32[8,32,1]{1,2,0:T(1,128)S(1)}, u32[]{:S(2)}, u32[]{:S(2)}) collective-permute-start(f32[8,32,1]{1,2,0:T(1,128)S(1)} %get-tuple-element.31), channel_id=1, source_target_pairs={{4,0},{8,4},{12,8},{16,12},{20,16},{24,20},{28,24},{5,1},{9,5},{13... | collective-permute-start | bytes 3080 | tf_op jit(solution)/shard_map/ppermute | solution.py:22
  189.6 10.6 %collective-permute-start.22 = (f32[8,1,66]{1,2,0:T(8,128)S(1)}, f32[8,1,66]{1,2,0:T(8,128)S(1)}, u32[]{:S(2)}, u32[]{:S(2)}) collective-permute-start(f32[8,1,66]{1,2,0:T(8,128)S(1)} %get-tuple-element.23), channel_id=1, source_target_pairs={{1,0},{2,1},{3,2},{5,4},{6,5},{7,6},{9,8},{10,9},{11,10},{13,12},{... | collective-permute-start | bytes 6344 | tf_op jit(solution)/shard_map/ppermute | solution.py:22
  190.9 11.0 %collective-permute-start.23 = (f32[8,1,66]{1,2,0:T(8,128)S(1)}, f32[8,1,66]{1,2,0:T(8,128)S(1)}, u32[]{:S(2)}, u32[]{:S(2)}) collective-permute-start(f32[8,1,66]{1,2,0:T(8,128)S(1)} %get-tuple-element.22), channel_id=1, source_target_pairs={{0,1},{1,2},{2,3},{4,5},{5,6},{6,7},{8,9},{9,10},{10,11},{12,13},{... | collective-permute-start | bytes 6344 | tf_op jit(solution)/shard_map/ppermute | solution.py:21
  220.1 3.6 %copy-start.12 = (bf16[32,32]{1,0:T(8,128)(2,1)S(1)}, bf16[32,32]{1,0:T(8,128)(2,1)}, u32[]{:S(2)}) copy-start(bf16[32,32]{1,0:T(8,128)(2,1)} %param.10) | copy-start | bytes 6148
  221.5 28.3 %copy-start.4 = (bf16[8,4,8,128]{3,2,1,0:T(8,128)(2,1)S(1)}, bf16[8,4,8,128]{3,2,1,0:T(8,128)(2,1)}, u32[]{:S(2)}) copy-start(bf16[8,4,8,128]{3,2,1,0:T(8,128)(2,1)} %param.8) | copy-start | bytes 196612
Sparse Core Ops, SparseCore 0:
  10.1 48.3 all-gather.1
  65.6 32.8 reduce-scatter.6
  225.1 24.6 reduce-scatter.4
where the time goes:
time: 259 us; the launch traced here: 258 us
  waiting for transfers between devices  136 us (53%)
  starting transfers between devices  58.4 us (23%)
  blocking collectives  17.4 us (7%)
  between operations  14.5 us (6%)
  local copies, waits for them, and re-layouts  11.8 us (5%)
  other arithmetic  10.6 us (4%)
  matrix products  9.04 us (3%)
    ppermute x12, starting transfers between devices, padded_2(): before = lax.ppermute(last, axis, up)  42.8 us
    all_gather x1, waiting for transfers between devices, body(): lax.all_gather(widened, 'lat', axis=0, tiled=True)  39.5 us
    ppermute x12, waiting for transfers between devices, padded_2(): after = lax.ppermute(initial, axis, down)  38.1 us
    reduce_scatter x1, waiting for transfers between devices, body(): lax.psum_scatter(jnp.einsum('rc,mlrw->cmlw', columns, projected, precisio...  24.8 us
    unnamed x4, waiting for transfers between devices  24.4 us
    all_gather x1, blocking collectives, body(): lax.all_gather(adjoint, 'mem', axis=2, tiled=True)[None]  17.4 us
    ppermute x12, starting transfers between devices, padded_2(): after = lax.ppermute(initial, axis, down)  15.5 us
    ppermute x12, waiting for transfers between devices, padded_2(): before = lax.ppermute(last, axis, up)  9.46 us
  transfers between devices with their start and end apart: 27, of which 19 were waited for; matrix products, arithmetic and copies ran while one was open for 6% of the time, Pallas kernels for 0%

commit v1 on v0

v1 whole, which is shorter than its diff:
```python
import functools

import jax
import jax.numpy as jnp
from jax import lax
from jax.experimental import pallas as pl
from jax.experimental.pallas import tpu as pltpu
from jax.sharding import PartitionSpec as P

STEPS = 4
OBLK = 8
HALO = 2 * STEPS
LANES = 128
DIFFUSION = 0.2
F32 = jnp.float32
BF16 = jnp.bfloat16


def split2(x):
    hi = x.astype(BF16)
    return hi, (x - hi.astype(F32)).astype(BF16)


def dot(a, b, dims=((1,), (0,))):
    return lax.dot_general(a, b, (dims, ((), ())), preferred_element_type=F32)


def kernel(
    nmem,
    nlat,
    scale,
    coarse_ref,
    pert_ref,
    lat_ref,
    lon_ref,
    aux_ref,
    band_ref,
    inc_ref,
    cg,
    auxg,
    part,
    pr,
    rs,
    ext,
    spread,
    coef,
    wts,
    vals,
    itile,
    incr,
    adjg,
    gb,
    gr,
    cg_ss,
    cg_rs,
    aux_ss,
    aux_rs,
    ah_ss,
    ah_rs,
    pr_ss,
    pr_rs,
    rs_ss,
    rs_rs,
    halo_ss,
    halo_rs,
    inc_ss,
    inc_rs,
    adj_ss,
    adj_rs,
    rel_ss,
    rel_rs,
    g_ss,
    g_rs,
):
    members, lev, rows, flon = pert_ref.shape
    clon = lon_ref.shape[0]
    cols = flon // nmem
    groups = nmem // lev
    urows = rows // groups
    erows = urows + 2 * HALO
    npairs = nmem // 2
    me = lax.axis_index("mem")
    z = lax.axis_index("lat")
    pair = me // 2
    core = me % 2
    partner = pair * 2 + (1 - core)
    my_level = me // groups
    my_group = me % groups
    my_row = my_group * urows
    block = z * groups + my_group
    has_up = block > 0
    has_down = block < nlat * groups - 1

    def neighbour(shift):
        there = block + shift
        return (my_level * groups + (there + groups) % groups, (there + groups) // groups - 1)

    up = neighbour(-1)
    down = neighbour(1)

    def send(src, dst, ss, rsem, mem, lat):
        return pltpu.make_async_remote_copy(
            src_ref=src,
            dst_ref=dst,
            send_sem=ss,
            recv_sem=rsem,
            device_id={"mem": mem, "lat": lat},
            device_id_type=pl.DeviceIdType.MESH,
        )

    barrier = pltpu.get_barrier_semaphore()

    def greet(mem, lat):
        pl.semaphore_signal(
            barrier, inc=1, device_id={"mem": mem, "lat": lat}, device_id_type=pl.DeviceIdType.MESH
        )

    for i in range(1, nmem):
        greet((me + i) % nmem, z)
    for i in range(1, nlat):
        greet(me, (z + i) % nlat)
    pl.semaphore_wait(barrier, nmem + nlat - 2)
    if groups > 1:
        far_up = has_up & (my_group == 0)
        far_down = has_down & (my_group == groups - 1)

        @pl.when(far_up)
        def _():
            greet(*up)

        @pl.when(far_down)
        def _():
            greet(*down)

        @pl.when(far_up)
        def _():
            pl.semaphore_wait(barrier, 1)

        @pl.when(far_down)
        def _():
            pl.semaphore_wait(barrier, 1)

    def cg_copy(there):
        return send(coarse_ref, cg.at[z], cg_ss.at[there], cg_rs.at[z], me, there)

    def cg_arrival(source):
        return send(coarse_ref, cg.at[source], cg_ss.at[source], cg_rs.at[source], me, source)

    for i in range(1, nlat):
        cg_copy((z + i) % nlat).start()

    def aux_copy(there):
        return send(
            aux_ref.at[there // groups, pl.ds(pl.multiple_of((there % groups) * urows, 8), urows)],
            auxg.at[me, pl.ds(HALO, urows)],
            aux_ss.at[there],
            aux_rs.at[me],
            there,
            z,
        )

    def aux_arrival(source):
        return send(
            aux_ref.at[0, pl.ds(0, urows)],
            auxg.at[source, pl.ds(HALO, urows)],
            aux_ss.at[source],
            aux_rs.at[source],
            source,
            z,
        )

    for i in range(1, nmem):
        aux_copy((me + i) % nmem).start()

    cg[z] = coarse_ref[...]
    auxg[me, HALO : HALO + urows] = aux_ref[my_level, pl.ds(pl.multiple_of(my_row, 8), urows)]

    @pl.when(jnp.logical_not(has_up))
    def _():
        auxg[:, :HALO] = jnp.zeros((nmem, HALO, 2 * LANES), F32)
        ext[:HALO] = jnp.zeros((HALO, flon), F32)

    @pl.when(jnp.logical_not(has_down))
    def _():
        auxg[:, HALO + urows :] = jnp.zeros((nmem, HALO, 2 * LANES), F32)
        ext[HALO + urows :] = jnp.zeros((HALO, flon), F32)

    per_tile = cols // OBLK
    k = lax.broadcasted_iota(jnp.int32, (2 * LANES, LANES), 0)
    n = lax.broadcasted_iota(jnp.int32, (2 * LANES, LANES), 1)
    for piece in range(3 * STEPS):
        hit = k == (n // cols) * LANES + piece * per_tile + (n % cols) // OBLK
        spread[:, piece * LANES : (piece + 1) * LANES] = jnp.where(hit, 1.0, 0.0).astype(BF16)

    lat_f32 = lat_ref[...].astype(F32)
    lat_bf = lat_ref[...]
    lat_t = jnp.transpose(lat_f32).astype(BF16)
    lat_t2 = jnp.concatenate([lat_t, lat_t], axis=1)
    lon = lon_ref[...]

    for i in range(1, nlat):
        cg_arrival((z + nlat - i) % nlat).wait_recv()

    def pr_copy(p):
        unit = 2 * p + (1 - core)
        return send(part.at[unit], pr.at[p], pr_ss.at[p], pr_rs.at[p], partner, z)

    def pr_arrival(p):
        return send(part.at[2 * p + core], pr.at[p], pr_ss.at[p], pr_rs.at[p], partner, z)

    def forward(i, carry):
        if groups == 1:
            half = lev // 2
            level = jnp.where(i < half, 2 * i + (1 - core), 2 * (i - half) + core)
        else:
            level = i
        coarse = jnp.concatenate(
            [cg[:, m, level].astype(F32).reshape(-1, clon) for m in range(members)], axis=1
        ).astype(BF16)
        partly = dot(lat_bf, coarse)
        partly = jnp.concatenate(
            [partly[:, m * clon : (m + 1) * clon] for m in range(members)], axis=0
        )
        hi, lo = split2(partly)
        localized = dot(hi, lon) + dot(lo, lon)
        total = localized[:rows] * pert_ref[0, level].astype(F32)
        for m in range(1, members):
            total += localized[m * rows : (m + 1) * rows] * pert_ref[m, level].astype(F32)
        part[pl.ds(level * groups, groups)] = total.reshape(groups, urows, flon)
        if groups == 1:

            @pl.when(i < lev // 2)
            def _():
                pr_copy(i).start()

        else:
            for g in range(groups // 2):
                pr_copy(level * (groups // 2) + g).start()
        return carry

    lax.fori_loop(0, lev, forward, 0)

    for i in range(1, nmem):
        aux_arrival((me + nmem - i) % nmem).wait_recv()
    ah_up = send(
        auxg.at[:, pl.ds(HALO, HALO)],
        auxg.at[:, pl.ds(HALO + urows, HALO)],
        ah_ss.at[0],
        ah_rs.at[0],
        *up,
    )
    ah_down = send(
        auxg.at[:, pl.ds(urows, HALO)], auxg.at[:, pl.ds(0, HALO)], ah_ss.at[1], ah_rs.at[1], *down
    )

    @pl.when(has_up)
    def _():
        ah_up.start()

    @pl.when(has_down)
    def _():
        ah_down.start()

    def rs_copy(p):
        return send(pr.at[p], rs.at[pair], rs_ss.at[p], rs_rs.at[pair], 2 * p + core, z)

    def rs_arrival(p):
        return send(pr.at[p], rs.at[p], rs_ss.at[p], rs_rs.at[p], 2 * p + core, z)

    def combine(i, carry):
        p = (pair + 1 + i) % npairs
        pr_arrival(p).wait_recv()
        pr[p] = pr[p] + part[2 * p + core]

        @pl.when(p != pair)
        def _():
            rs_copy(p).start()

        return carry

    lax.fori_loop(0, npairs, combine, 0)

    @pl.when(has_down)
    def _():
        ah_up_arrival = send(
            auxg.at[:, pl.ds(HALO, HALO)],
            auxg.at[:, pl.ds(HALO + urows, HALO)],
            ah_ss.at[0],
            ah_rs.at[0],
            *down,
        )
        ah_up_arrival.wait_recv()

    @pl.when(has_up)
    def _():
        ah_down_arrival = send(
            auxg.at[:, pl.ds(urows, HALO)],
            auxg.at[:, pl.ds(0, HALO)],
            ah_ss.at[1],
            ah_rs.at[1],
            *up,
        )
        ah_down_arrival.wait_recv()

    @pl.when(has_up)
    def _():
        ah_up.wait_send()

    @pl.when(has_down)
    def _():
        ah_down.wait_send()

    place = block * urows - HALO + lax.broadcasted_iota(jnp.int32, (erows, LANES), 0)
    inside = (place >= 0) & (place < nlat * rows)
    lane = lax.broadcasted_iota(jnp.int32, (erows, LANES), 1)
    tiles = LANES // cols
    for q in range(flon // LANES):
        first, second = auxg[tiles * q], auxg[tiles * q + 1]
        lhs = jnp.concatenate([first[:, :LANES], second[:, :LANES]], axis=1)
        hi, rest = lhs.astype(BF16), lhs
        rest = rest - hi.astype(F32)
        mid, low = split2(rest)
        out = dot(jnp.concatenate([hi, mid, low], axis=0), spread[...])
        out = out[:erows] + out[erows : 2 * erows] + out[2 * erows :]
        at = slice(q * LANES, (q + 1) * LANES)
        for t in range(STEPS):
            weight = out[:, t * LANES : (t + 1) * LANES]
            value = out[:, (STEPS + t) * LANES : (STEPS + t + 1) * LANES]
            cell = out[:, (2 * STEPS + t) * LANES : (2 * STEPS + t + 1) * LANES]
            hit = cell == (lane % OBLK).astype(F32)
            wts[t, :, at] = jnp.where(hit, weight, 0.0)
            vals[t, :, at] = value
        w0, w1 = first[:, LANES:], second[:, LANES:]
        lower = lane < cols
        c0 = jnp.where(lower, w0, pltpu.roll(w1, cols, 1))
        c1 = jnp.where(lower, pltpu.roll(w0, cols, 1), w1)
        east_in = inside & (lane + q * LANES < flon - 1)
        west_in = inside & (lane + q * LANES > 0)
        coef[0, :, at] = jnp.where(inside, DIFFUSION - 0.5 * c1, 0.0)
        coef[1, :, at] = jnp.where(inside, DIFFUSION + 0.5 * c1, 0.0)
        coef[2, :, at] = jnp.where(east_in, DIFFUSION - 0.5 * c0, 0.0)
        coef[3, :, at] = jnp.where(west_in, DIFFUSION + 0.5 * c0, 0.0)
        coef[4, :, at] = jnp.where(inside, jnp.full((erows, LANES), 1.0 - 4.0 * DIFFUSION, F32), 0.0)

    total = pr[pair]
    for i in range(1, npairs):
        p = (pair + npairs - i) % npairs
        rs_arrival(p).wait_recv()
        total = total + rs[p]
    total = total * scale
    ext[HALO : HALO + urows] = total
    halo_up = send(
        ext.at[pl.ds(HALO, HALO)],
        ext.at[pl.ds(HALO + urows, HALO)],
        halo_ss.at[0],
        halo_rs.at[0],
        *up,
    )
    halo_down = send(
        ext.at[pl.ds(urows, HALO)], ext.at[pl.ds(0, HALO)], halo_ss.at[1], halo_rs.at[1], *down
    )

    @pl.when(has_up)
    def _():
        halo_up.start()

    @pl.when(has_down)
    def _():
        halo_down.start()

    for m in range(nmem):
        itile[m] = total[:, m * cols : (m + 1) * cols]

    def inc_copy(there):
        return send(
            itile.at[there],
            incr.at[my_level, pl.ds(pl.multiple_of(my_row, 8), urows)],
            inc_ss.at[there],
            inc_rs.at[me],
            there,
            z,
        )

    def inc_arrival(source):
        return send(
            itile.at[source],
            incr.at[
                source // groups, pl.ds(pl.multiple_of((source % groups) * urows, 8), urows)
            ],
            inc_ss.at[source],
            inc_rs.at[source],
            source,
            z,
        )

    for i in range(1, nmem):
        inc_copy((me + i) % nmem).start()
    incr[my_level, pl.ds(pl.multiple_of(my_row, 8), urows)] = itile[me]

    @pl.when(has_down)
    def _():
        send(
            ext.at[pl.ds(HALO, HALO)],
            ext.at[pl.ds(HALO + urows, HALO)],
            halo_ss.at[0],
            halo_rs.at[0],
            *down,
        ).wait_recv()

    @pl.when(has_up)
    def _():
        send(
            ext.at[pl.ds(urows, HALO)], ext.at[pl.ds(0, HALO)], halo_ss.at[1], halo_rs.at[1], *up
        ).wait_recv()

    @pl.when(has_up)
    def _():
        halo_up.wait_send()

    @pl.when(has_down)
    def _():
        halo_down.wait_send()

    state = ext[...]
    forcing = []
    for t in range(STEPS):
        state = (
            coef[4] * state
            + coef[0] * pltpu.roll(state, erows - 1, 0)
            + coef[1] * pltpu.roll(state, 1, 0)
            + coef[2] * pltpu.roll(state, flon - 1, 1)
            + coef[3] * pltpu.roll(state, 1, 1)
        )
        wts[t] = wts[t] * (state - vals[t])
    adjoint = None
    for t in reversed(range(STEPS)):
        adjoint = wts[t] if adjoint is None else adjoint + wts[t]
        adjoint = (
            coef[4] * adjoint
            + pltpu.roll(coef[1] * adjoint, erows - 1, 0)
            + pltpu.roll(coef[0] * adjoint, 1, 0)
            + pltpu.roll(coef[3] * adjoint, flon - 1, 1)
            + pltpu.roll(coef[2] * adjoint, 1, 1)
        )
    adjg[me] = adjoint[HALO : HALO + urows]

    def adj_copy(p):
        return send(adjg.at[me], adjg.at[me], adj_ss.at[p], adj_rs.at[pair], 2 * p + core, z)

    def adj_arrival(p):
        unit = 2 * p + core
        return send(adjg.at[unit], adjg.at[unit], adj_ss.at[p], adj_rs.at[p], unit, z)

    def relay(p):
        unit = 2 * p + core
        return send(adjg.at[unit], adjg.at[unit], rel_ss.at[p], rel_rs.at[p], partner, z)

    def relay_arrival(p):
        unit = 2 * p + (1 - core)
        return send(adjg.at[unit], adjg.at[unit], rel_ss.at[p], rel_rs.at[p], partner, z)

    for i in range(1, npairs):
        adj_copy((pair + i) % npairs).start()

    def g_copy(there, level):
        return send(
            gb.at[there, level], gr.at[z, level], g_ss.at[there, level], g_rs.at[z, level], me, there
        )

    def g_arrival(source, level):
        return send(
            gb.at[source, level],
            gr.at[source, level],
            g_ss.at[source, level],
            g_rs.at[source, level],
            me,
            source,
        )

    def backward(level):
        field = adjg[pl.ds(level * groups, groups)].reshape(rows, flon)
        product = jnp.concatenate(
            [pert_ref[m, level].astype(F32) * field for m in range(members)], axis=0
        )
        hi, lo = split2(product)
        over_lon = ((1,), (1,))
        projected = dot(hi, lon, over_lon) + dot(lo, lon, over_lon)
        projected = jnp.concatenate(
            [projected[m * rows : (m + 1) * rows] for m in range(members)], axis=1
        )
        hi, lo = split2(projected)
        banded = dot(lat_t2, jnp.concatenate([hi, lo], axis=0))
        gb[:, level] = banded.reshape(nlat, -1, members * clon)
        for i in range(1, nlat):
            g_copy((z + i) % nlat, level).start()

    def near(i, carry):
        p = (pair + npairs - i) % npairs

        @pl.when(i > 0)
        def _():
            adj_arrival(p).wait_recv()

        relay(p).start()
        if groups == 1:
            backward(2 * p + core)
        return carry

    lax.fori_loop(0, npairs, near, 0)

    def far(i, carry):
        p = (pair + npairs - i) % npairs
        relay_arrival(p).wait_recv()
        if groups == 1:
            backward(2 * p + (1 - core))
        elif groups == 2:
            backward(p)
        else:

            @pl.when(p % (groups // 2) == groups // 2 - 1)
            def _():
                backward(p // (groups // 2))

        return carry

    lax.fori_loop(0, npairs, far, 0)

    for i in range(1, nmem):
        inc_arrival((me + nmem - i) % nmem).wait_recv()
    inc_ref[...] = incr[...]

    def finish(level, carry):
        total = gb[z, level]
        for i in range(1, nlat):
            source = (z + nlat - i) % nlat
            g_arrival(source, level).wait_recv()
            total = total + gr[source, level]
        band_ref[level] = total
        return carry

    lax.fori_loop(0, lev, finish, 0)

    for i in range(1, nlat):
        cg_copy((z + i) % nlat).wait_send()
    for i in range(1, nmem):
        aux_copy((me + i) % nmem).wait_send()
        inc_copy((me + i) % nmem).wait_send()
    for p in range(npairs):
        pr_copy(p).wait_send()
        relay(p).wait_send()
    for i in range(1, npairs):
        rs_copy((pair + i) % npairs).wait_send()
        adj_copy((pair + i) % npairs).wait_send()

    def drain(level, carry):
        for i in range(1, nlat):
            g_copy((z + i) % nlat, level).wait_send()
        return carry

    lax.fori_loop(0, lev, drain, 0)


def body(
    nmem,
    nlat,
    coarse_weights,
    perturbations,
    lat_matrix,
    lon_matrix,
    wind_field,
    observed_cell,
    observed_value,
    observed_weight,
):
    members, lev, rows, flon = perturbations.shape
    cband, _, _, clon = coarse_weights.shape
    cols = wind_field.shape[2]
    blocks = cols // OBLK
    groups = nmem // lev
    urows = rows // groups
    erows = urows + 2 * HALO
    npairs = nmem // 2
    assert nmem == lev * groups and nmem % 2 == 0 and urows % 8 == 0 and urows >= HALO
    assert 2 * cols == LANES and 3 * STEPS * blocks <= LANES
    scale = 1.0 / jnp.sqrt(jnp.float32(members * nmem - 1))
    coarse_t = jnp.transpose(coarse_weights, (1, 2, 0, 3))
    obs = jnp.stack([observed_weight, observed_value, observed_cell.astype(F32)])
    obs = jnp.transpose(obs, (2, 3, 0, 1, 4)).reshape(lev, rows, 3 * STEPS * blocks)
    obs = jnp.pad(obs, ((0, 0), (0, 0), (0, LANES - obs.shape[2])))
    wind = jnp.transpose(wind_field, (1, 0, 2)).reshape(1, rows, 2 * cols)
    aux = jnp.concatenate([obs, jnp.broadcast_to(wind, (lev, rows, LANES))], axis=2)
    vmem = pl.BlockSpec(memory_space=pltpu.VMEM)
    dma = pltpu.SemaphoreType.DMA
    width = members * clon
    banded, increment = pl.pallas_call(
        functools.partial(kernel, nmem, nlat, float(1.0 / (members * nmem - 1) ** 0.5)),
        out_shape=(
            jax.ShapeDtypeStruct((lev, cband, width), F32),
            jax.ShapeDtypeStruct((lev, rows, cols), F32),
        ),
        in_specs=[vmem] * 5,
        out_specs=(vmem, vmem),
        scratch_shapes=[
            pltpu.VMEM((nlat, members, lev, cband, clon), BF16),
            pltpu.VMEM((nmem, erows, 2 * LANES), F32),
            pltpu.VMEM((nmem, urows, flon), F32),
            pltpu.VMEM((npairs, urows, flon), F32),
            pltpu.VMEM((npairs, urows, flon), F32),
            pltpu.VMEM((erows, flon), F32),
            pltpu.VMEM((2 * LANES, 3 * STEPS * LANES), BF16),
            pltpu.VMEM((5, erows, flon), F32),
            pltpu.VMEM((STEPS, erows, flon), F32),
            pltpu.VMEM((STEPS, erows, flon), F32),
            pltpu.VMEM((nmem, urows, cols), F32),
            pltpu.VMEM((lev, rows, cols), F32),
            pltpu.VMEM((nmem, urows, flon), F32),
            pltpu.VMEM((nlat, lev, cband, width), F32),
            pltpu.VMEM((nlat, lev, cband, width), F32),
            dma((nlat,)),
            dma((nlat,)),
            dma((nmem,)),
            dma((nmem,)),
            dma((2,)),
            dma((2,)),
            dma((npairs,)),
            dma((npairs,)),
            dma((npairs,)),
            dma((npairs,)),
            dma((2,)),
            dma((2,)),
            dma((nmem,)),
            dma((nmem,)),
            dma((npairs,)),
            dma((npairs,)),
            dma((npairs,)),
            dma((npairs,)),
            dma((nlat, lev)),
            dma((nlat, lev)),
        ],
        compiler_params=pltpu.CompilerParams(
            collective_id=0, has_side_effects=True, vmem_limit_bytes=60 * 1024 * 1024
        ),
    )(coarse_t, perturbations, lat_matrix, lon_matrix, aux)
    banded = jnp.transpose(banded.reshape(lev, cband, members, clon), (1, 2, 0, 3))
    return banded * scale + coarse_weights.astype(F32), increment


def solution(mesh):
    in_specs = (
        P("lat", "mem", None, None),
        P("mem", None, "lat", None),
        P("lat", None),
        P(),
        P(None, "lat", "mem"),
        P(None, None, "lat", "mem"),
        P(None, None, "lat", "mem"),
        P(None, None, "lat", "mem"),
    )
    out_specs = (P("lat", "mem", None, None), P(None, "lat", "mem"))
    call = functools.partial(body, mesh.shape["mem"], mesh.shape["lat"])
    return jax.shard_map(call, mesh=mesh, in_specs=in_specs, out_specs=out_specs, check_vma=False)
```

time: 259 us -> 48.1 us (0.19)
  waiting for transfers between devices: 136 us -> 0 us
  starting transfers between devices: 58.4 us -> 0 us
  Pallas kernels: 0 us -> 41.1 us
  blocking collectives: 17.4 us -> 0 us
  between operations: 14.5 us -> 0.72 us
  local copies, waits for them, and re-layouts: 11.8 us -> 2.55 us
  matrix products: 9.04 us -> 0 us
  other arithmetic: 10.6 us -> 3.37 us
    ppermute x24 -> x0, starting transfers between devices: 58.3 us -> none  [the longest x12 42.8 us: padded_2(): before = lax.ppermute(last, axis, up)]
    ppermute x24 -> x0, waiting for transfers between devices: 47.5 us -> none  [the longest x12 38.1 us: padded_2(): after = lax.ppermute(initial, axis, down)]
    pallas_call x0 -> x1, Pallas kernels: none -> 41.1 us  [body(): pl.pallas_call(functools.partial(kernel, nmem, nlat, float(1.0 / (members...]
    all_gather x1 -> x0, waiting for transfers between devices: 39.5 us -> none  [body(): lax.all_gather(widened, 'lat', axis=0, tiled=True)]
    reduce_scatter x1 -> x0, waiting for transfers between devices: 24.8 us -> none  [body(): lax.psum_scatter(jnp.einsum('rc,mlrw->cmlw', columns, projected, precisio...]
    unnamed x4 -> x0, waiting for transfers between devices: 24.4 us -> none
    all_gather x1 -> x0, blocking collectives: 17.4 us -> none  [body(): lax.all_gather(adjoint, 'mem', axis=2, tiled=True)[None]]
    dot_general x4 -> x0, matrix products: 9.04 us -> none  [the longest x1 3.72 us: body(): jnp.einsum('rc,cmlf->mlrf', columns, lax.all_gather(widened, 'lat', axis=...]
  transfers between devices with their start and end apart: 27 -> 0, of which waited for: 19 -> 0; matrix products, arithmetic and copies ran while one was open for 6% -> 0% of each run, Pallas kernels for 0% -> 0%
where the time goes in v1:
time: 48.1 us; the launch traced here: 47.8 us
  Pallas kernels  41.1 us (85%)
  other arithmetic  3.37 us (7%)
  local copies, waits for them, and re-layouts  2.55 us (5%)
  between operations  0.72 us (1%)
    pallas_call x1, Pallas kernels, body(): pl.pallas_call(functools.partial(kernel, nmem, nlat, float(1.0 / (members...  41.1 us
    unnamed x12, local copies, waits for them, and re-layouts  2.24 us

profile of v1, /device:TPU:0, one launch (start us, length us, event | category | flops | bytes accessed | tf_op | source)
XLA Modules:
  0.0 47.8 jit_solution(728371452315926469)
XLA Ops:
  0.6 0.0 copy-start.3
  0.6 0.0 copy-start.2
  0.7 1.0 %convert_bitcast_fusion = f32[1,4,8,32,8]{3,4,2,1,0:T(8,128)S(1)} fusion(s32[4,8,32,8]{2,3,1,0:T(8,128)} %param.13), kind=kLoop, calls=%fused_computation.5 | loop fusion | flops 8192 | bytes 65536 | tf_op jit(solution)/shard_map/stack | solution.py:587
  1.6 0.0 copy-done.3
  1.6 0.0 copy-done.2
  1.7 0.0 copy-start.4
  1.8 0.1 copy.15
  1.9 0.6 %copy-done.4 = f32[2,32,64]{2,1,0:T(8,128)S(1)} copy-done((f32[2,32,64]{2,1,0:T(8,128)S(1)}, f32[2,32,64]{2,1,0:T(8,128)}, u32[]{:S(2)}) %copy-start.4) | copy-done | bytes 16408
  2.5 0.1 broadcast_in_dim.7
  2.6 0.0 copy-start
  2.7 0.7 %select_maximum_fusion.aux_ref = f32[8,32,256]{2,1,0:T(8,128)} fusion(f32[8,32,96]{2,1,0:T(8,128)S(1)} %copy.15, f32[8,32,128]{2,1,0:T(8,128)S(1)} %broadcast_in_dim.8), kind=kLoop, calls=%fused_computation.1 | loop fusion | flops 196608 | bytes 491520 | tf_op jit(solution)/shard_map/concatenate | solution.py:591
  3.4 0.1 copy-done
  3.5 0.7 %copy.20 = bf16[8,4,8,128]{3,0,2,1:T(8,128)(2,1)} copy(bf16[8,4,8,128]{3,2,1,0:T(8,128)(2,1)S(1)} %copy-done) | data formatting | bytes 131072 | tf_op args[0]
  4.1 41.1 %shard_map.95 = (f32[8,8,512]{2,1,0:T(8,128)}, f32[8,32,64]{2,1,0:T(8,128)}) custom-call(bf16[4,8,8,128]{3,2,1,0:T(8,128)(2,1)} %bitcast.16, bf16[4,8,32,512]{3,2,1,0:T(8,128)(2,1)} %pert_ref.1, bf16[32,32]{1,0:T(8,128)(2,1)} %lat_ref.1, bf16[128,512]{1,0:T(8,128)(2,1)} %lon_ref.1, f32[8,32,256]{2,1,0:T(8,128)} %select_maximum_fusion.aux_ref), custom_call_target="tpu_custom_call" | custom-call | tf_op jit(solution)/shard_map/pallas_call | solution.py:595
  45.3 0.9 %multiply_bitcast_fusion = f32[8,8,4,128]{3,1,2,0:T(8,128)S(1)} fusion(f32[8,8,512]{2,1,0:T(8,128)} %get-tuple-element.4), kind=kLoop, calls=%fused_computation.4 | loop fusion | flops 32768 | bytes 262144 | tf_op jit(solution)/shard_map/mul | solution.py:645
  46.2 0.0 copy-start.1
  46.2 0.7 %bitcast_add_fusion = f32[8,4,8,128]{3,2,1,0:T(8,128)} fusion(f32[8,8,4,128]{3,1,2,0:T(8,128)S(1)} %multiply_bitcast_fusion, bf16[8,4,8,128]{3,2,1,0:T(8,128)(2,1)S(1)} %copy-done), kind=kLoop, calls=%fused_computation.3 | loop fusion | flops 65536 | bytes 327680 | tf_op jit(solution)/shard_map/add | solution.py:645
  46.9 0.2 copy-done.1
  47.1 0.7 %copy.22 = f32[8,32,64]{2,1,0:T(8,128)} copy(f32[8,32,64]{2,1,0:T(8,128)S(1)} %copy-done.1) | data formatting | bytes 131072
  (4 shorter events, 0.1 us)
Async XLA Ops:
  0.6 1.0 %copy-start.3 = (f32[4,8,32,8]{2,3,1,0:T(8,128)S(1)}, f32[4,8,32,8]{2,3,1,0:T(8,128)}, u32[]{:S(2)}) copy-start(f32[4,8,32,8]{2,3,1,0:T(8,128)} %param.15) | copy-start | bytes 98308
  0.6 1.0 %copy-start.2 = (f32[4,8,32,8]{2,3,1,0:T(8,128)S(1)}, f32[4,8,32,8]{2,3,1,0:T(8,128)}, u32[]{:S(2)}) copy-start(f32[4,8,32,8]{2,3,1,0:T(8,128)} %param.14) | copy-start | bytes 98308
  1.7 0.8 %copy-start.4 = (f32[2,32,64]{2,1,0:T(8,128)S(1)}, f32[2,32,64]{2,1,0:T(8,128)}, u32[]{:S(2)}) copy-start(f32[2,32,64]{2,1,0:T(8,128)} %param.12) | copy-start | bytes 49156
  2.6 0.8 %copy-start = (bf16[8,4,8,128]{3,2,1,0:T(8,128)(2,1)S(1)}, bf16[8,4,8,128]{3,2,1,0:T(8,128)(2,1)}, u32[]{:S(2)}) copy-start(bf16[8,4,8,128]{3,2,1,0:T(8,128)(2,1)} %param.8) | copy-start | bytes 196612
  46.2 0.9 %copy-start.1 = (f32[8,32,64]{2,1,0:T(8,128)S(1)}, f32[8,32,64]{2,1,0:T(8,128)}, u32[]{:S(2)}) copy-start(f32[8,32,64]{2,1,0:T(8,128)} %get-tuple-element.9) | copy-start | bytes 196612

commit v2 on v1

--- a/solution.py
+++ b/solution.py
@@ -29,13 +29,25 @@
     nmem,
     nlat,
     scale,
+    coarse_hbm,
+    pert_hbm,
+    lat_hbm,
+    lon_hbm,
+    wind_hbm,
+    cell_hbm,
+    value_hbm,
+    weight_hbm,
+    grad_ref,
+    inc_ref,
     coarse_ref,
     pert_ref,
     lat_ref,
     lon_ref,
+    wind_ref,
+    cell_ref,
+    value_ref,
+    weight_ref,
     aux_ref,
-    band_ref,
-    inc_ref,
     cg,
     auxg,
     part,
@@ -51,6 +63,7 @@
     adjg,
     gb,
     gr,
+    in_sem,
     cg_ss,
     cg_rs,
     aux_ss,
@@ -108,6 +121,22 @@
             device_id_type=pl.DeviceIdType.MESH,
         )
 
+    arguments = (
+        (coarse_hbm, coarse_ref),
+        (lat_hbm, lat_ref),
+        (lon_hbm, lon_ref),
+        (wind_hbm, wind_ref),
+        (cell_hbm, cell_ref),
+        (value_hbm, value_ref),
+        (weight_hbm, weight_ref),
+        (pert_hbm, pert_ref),
+    )
+    loads = [
+        pltpu.make_async_copy(src, dst, in_sem.at[i]) for i, (src, dst) in enumerate(arguments)
+    ]
+    for load in loads:
+        load.start()
+
     barrier = pltpu.get_barrier_semaphore()
 
     def greet(mem, lat):
@@ -115,10 +144,15 @@
             barrier, inc=1, device_id={"mem": mem, "lat": lat}, device_id_type=pl.DeviceIdType.MESH
         )
 
+    for i in range(1, nlat):
+        greet(me, (z + i) % nlat)
     for i in range(1, nmem):
         greet((me + i) % nmem, z)
-    for i in range(1, nlat):
-        greet(me, (z + i) % nlat)
+    loads[0].wait()
+    for m in range(members):
+        mine = jnp.swapaxes(coarse_ref[:, m].astype(F32), 0, 1).astype(BF16)
+        for level in range(lev):
+            cg[z, level, m] = mine[level]
     pl.semaphore_wait(barrier, nmem + nlat - 2)
     if groups > 1:
         far_up = has_up & (my_group == 0)
@@ -140,14 +174,49 @@
         def _():
             pl.semaphore_wait(barrier, 1)
 
-    def cg_copy(there):
-        return send(coarse_ref, cg.at[z], cg_ss.at[there], cg_rs.at[z], me, there)
-
-    def cg_arrival(source):
-        return send(coarse_ref, cg.at[source], cg_ss.at[source], cg_rs.at[source], me, source)
-
-    for i in range(1, nlat):
-        cg_copy((z + i) % nlat).start()
+    def level_at(i):
+        if groups > 1:
+            return i
+        half = lev // 2
+        p = (pair + 1 + i) % npairs
+        return 2 * p + jnp.where(i < half, 1 - core, core)
+
+    def cg_copy(there, level):
+        return send(
+            cg.at[z, level], cg.at[z, level], cg_ss.at[there, level], cg_rs.at[z, level], me, there
+        )
+
+    def cg_arrival(source, level):
+        return send(
+            cg.at[source, level],
+            cg.at[source, level],
+            cg_ss.at[source, level],
+            cg_rs.at[source, level],
+            me,
+            source,
+        )
+
+    def spread_coarse(i, carry):
+        for j in range(1, nlat):
+            cg_copy((z + j) % nlat, level_at(i)).start()
+        return carry
+
+    lax.fori_loop(0, lev, spread_coarse, 0)
+
+    for load in loads[1:-1]:
+        load.wait()
+
+    blank = jnp.zeros((rows, LANES - 3 * STEPS * (cols // OBLK)), F32)
+    winds = jnp.concatenate([wind_ref[0], wind_ref[1]], axis=1)
+
+    def pack(level, carry):
+        pieces = [ref[t, level] for ref in (weight_ref, value_ref) for t in range(STEPS)]
+        pieces += [cell_ref[t, level].astype(F32) for t in range(STEPS)]
+        aux_ref[level, :, :LANES] = jnp.concatenate(pieces + [blank], axis=1)
+        aux_ref[level, :, LANES:] = winds
+        return carry
+
+    lax.fori_loop(0, lev, pack, 0)
 
     def aux_copy(there):
         return send(
@@ -172,7 +241,6 @@
     for i in range(1, nmem):
         aux_copy((me + i) % nmem).start()
 
-    cg[z] = coarse_ref[...]
     auxg[me, HALO : HALO + urows] = aux_ref[my_level, pl.ds(pl.multiple_of(my_row, 8), urows)]
 
     @pl.when(jnp.logical_not(has_up))
@@ -198,8 +266,7 @@
     lat_t2 = jnp.concatenate([lat_t, lat_t], axis=1)
     lon = lon_ref[...]
 
-    for i in range(1, nlat):
-        cg_arrival((z + nlat - i) % nlat).wait_recv()
+    loads[-1].wait()
 
     def pr_copy(p):
         unit = 2 * p + (1 - core)
@@ -208,14 +275,29 @@
     def pr_arrival(p):
         return send(part.at[2 * p + core], pr.at[p], pr_ss.at[p], pr_rs.at[p], partner, z)
 
+    def rs_copy(p):
+        return send(pr.at[p], rs.at[pair], rs_ss.at[p], rs_rs.at[pair], 2 * p + core, z)
+
+    def rs_arrival(p):
+        return send(pr.at[p], rs.at[p], rs_ss.at[p], rs_rs.at[p], 2 * p + core, z)
+
+    def combine(i, carry):
+        p = (pair + 1 + i) % npairs
+        pr_arrival(p).wait_recv()
+        pr[p] = pr[p] + part[2 * p + core]
+
+        @pl.when(p != pair)
+        def _():
+            rs_copy(p).start()
+
+        return carry
+
     def forward(i, carry):
-        if groups == 1:
-            half = lev // 2
-            level = jnp.where(i < half, 2 * i + (1 - core), 2 * (i - half) + core)
-        else:
-            level = i
+        level = level_at(i)
+        for j in range(1, nlat):
+            cg_arrival((z + nlat - j) % nlat, level).wait_recv()
         coarse = jnp.concatenate(
-            [cg[:, m, level].astype(F32).reshape(-1, clon) for m in range(members)], axis=1
+            [cg[:, level, m].astype(F32).reshape(-1, clon) for m in range(members)], axis=1
         ).astype(BF16)
         partly = dot(lat_bf, coarse)
         partly = jnp.concatenate(
@@ -231,7 +313,11 @@
 
             @pl.when(i < lev // 2)
             def _():
-                pr_copy(i).start()
+                pr_copy((pair + 1 + i) % npairs).start()
+
+            @pl.when(i >= lev // 2)
+            def _():
+                combine(i - lev // 2, 0)
 
         else:
             for g in range(groups // 2):
@@ -261,24 +347,8 @@
     def _():
         ah_down.start()
 
-    def rs_copy(p):
-        return send(pr.at[p], rs.at[pair], rs_ss.at[p], rs_rs.at[pair], 2 * p + core, z)
-
-    def rs_arrival(p):
-        return send(pr.at[p], rs.at[p], rs_ss.at[p], rs_rs.at[p], 2 * p + core, z)
-
-    def combine(i, carry):
-        p = (pair + 1 + i) % npairs
-        pr_arrival(p).wait_recv()
-        pr[p] = pr[p] + part[2 * p + core]
-
-        @pl.when(p != pair)
-        def _():
-            rs_copy(p).start()
-
-        return carry
-
-    lax.fori_loop(0, npairs, combine, 0)
+    if groups > 1:
+        lax.fori_loop(0, npairs, combine, 0)
 
     @pl.when(has_down)
     def _():
@@ -535,13 +605,14 @@
             source = (z + nlat - i) % nlat
             g_arrival(source, level).wait_recv()
             total = total + gr[source, level]
-        band_ref[level] = total
+        gb[z, level] = total
         return carry
 
     lax.fori_loop(0, lev, finish, 0)
-
-    for i in range(1, nlat):
-        cg_copy((z + i) % nlat).wait_send()
+    for m in range(members):
+        total = jnp.swapaxes(gb[z, :, :, m * clon : (m + 1) * clon], 0, 1)
+        grad_ref[:, m] = total * scale + coarse_ref[:, m].astype(F32)
+
     for i in range(1, nmem):
         aux_copy((me + i) % nmem).wait_send()
         inc_copy((me + i) % nmem).wait_send()
@@ -554,6 +625,7 @@
 
     def drain(level, carry):
         for i in range(1, nlat):
+            cg_copy((z + i) % nlat, level).wait_send()
             g_copy((z + i) % nlat, level).wait_send()
         return carry
 
@@ -582,26 +654,31 @@
     npairs = nmem // 2
     assert nmem == lev * groups and nmem % 2 == 0 and urows % 8 == 0 and urows >= HALO
     assert 2 * cols == LANES and 3 * STEPS * blocks <= LANES
-    scale = 1.0 / jnp.sqrt(jnp.float32(members * nmem - 1))
-    coarse_t = jnp.transpose(coarse_weights, (1, 2, 0, 3))
-    obs = jnp.stack([observed_weight, observed_value, observed_cell.astype(F32)])
-    obs = jnp.transpose(obs, (2, 3, 0, 1, 4)).reshape(lev, rows, 3 * STEPS * blocks)
-    obs = jnp.pad(obs, ((0, 0), (0, 0), (0, LANES - obs.shape[2])))
-    wind = jnp.transpose(wind_field, (1, 0, 2)).reshape(1, rows, 2 * cols)
-    aux = jnp.concatenate([obs, jnp.broadcast_to(wind, (lev, rows, LANES))], axis=2)
     vmem = pl.BlockSpec(memory_space=pltpu.VMEM)
     dma = pltpu.SemaphoreType.DMA
     width = members * clon
-    banded, increment = pl.pallas_call(
+    arguments = (
+        coarse_weights,
+        perturbations,
+        lat_matrix,
+        lon_matrix,
+        wind_field,
+        observed_cell,
+        observed_value,
+        observed_weight,
+    )
+    return pl.pallas_call(
         functools.partial(kernel, nmem, nlat, float(1.0 / (members * nmem - 1) ** 0.5)),
         out_shape=(
-            jax.ShapeDtypeStruct((lev, cband, width), F32),
+            jax.ShapeDtypeStruct((cband, members, lev, clon), F32),
             jax.ShapeDtypeStruct((lev, rows, cols), F32),
         ),
-        in_specs=[vmem] * 5,
+        in_specs=[pl.BlockSpec(memory_space=pl.ANY)] * len(arguments),
         out_specs=(vmem, vmem),
         scratch_shapes=[
-            pltpu.VMEM((nlat, members, lev, cband, clon), BF16),
+            *[pltpu.VMEM(x.shape, x.dtype) for x in arguments],
+            pltpu.VMEM((lev, rows, 2 * LANES), F32),
+            pltpu.VMEM((nlat, lev, members, cband, clon), BF16),
             pltpu.VMEM((nmem, erows, 2 * LANES), F32),
             pltpu.VMEM((nmem, urows, flon), F32),
             pltpu.VMEM((npairs, urows, flon), F32),
@@ -616,8 +693,9 @@
             pltpu.VMEM((nmem, urows, flon), F32),
             pltpu.VMEM((nlat, lev, cband, width), F32),
             pltpu.VMEM((nlat, lev, cband, width), F32),
-            dma((nlat,)),
-            dma((nlat,)),
+            dma((len(arguments),)),
+            dma((nlat, lev)),
+            dma((nlat, lev)),
             dma((nmem,)),
             dma((nmem,)),
             dma((2,)),
@@ -640,9 +718,7 @@
         compiler_params=pltpu.CompilerParams(
             collective_id=0, has_side_effects=True, vmem_limit_bytes=60 * 1024 * 1024
         ),
-    )(coarse_t, perturbations, lat_matrix, lon_matrix, aux)
-    banded = jnp.transpose(banded.reshape(lev, cband, members, clon), (1, 2, 0, 3))
-    return banded * scale + coarse_weights.astype(F32), increment
+    )(*arguments)
 
 
 def solution(mesh):

time: 48.1 us -> 45.2 us (0.940)
  local copies, waits for them, and re-layouts: 2.55 us -> 6.27 us
  other arithmetic: 3.37 us -> 0 us
  Pallas kernels: 41.1 us -> 38.1 us
    unnamed x12 -> x11, local copies, waits for them, and re-layouts: 2.24 us -> 6.27 us
    pallas_call x1, Pallas kernels: 41.1 us -> 38.1 us  [body(): pl.pallas_call(functools.partial(kernel, nmem, nlat, float(1.0 / (members...]
    another operation x1 -> x0, other arithmetic: 0.96 us -> none  [body(): jnp.stack([observed_weight, observed_value, observed_cell.astype(F32)])]
    mul x1 -> x0, other arithmetic: 0.92 us -> none  [body(): return (banded * scale + coarse_weights.astype(F32), increment)]
    add x1 -> x0, other arithmetic: 0.74 us -> none  [body(): return (banded * scale + coarse_weights.astype(F32), increment)]
    concatenate x1 -> x0, other arithmetic: 0.72 us -> none  [body(): jnp.concatenate([obs, jnp.broadcast_to(wind, (lev, rows, LANES))], axis=2)]
where the time goes in v2:
time: 45.2 us; the launch traced here: 45.1 us
  Pallas kernels  38.1 us (84%)
  local copies, waits for them, and re-layouts  6.27 us (14%)
  between operations  0.66 us (1%)
    pallas_call x1, Pallas kernels, body(): pl.pallas_call(functools.partial(kernel, nmem, nlat, float(1.0 / (members...  38.1 us
    unnamed x11, local copies, waits for them, and re-layouts  6.27 us

profile of v2, /device:TPU:0, one launch (start us, length us, event | category | flops | bytes accessed | tf_op | source)
XLA Modules:
  0.0 45.1 jit_solution(12512716661484954220)
XLA Ops:
  0.6 0.0 copy-start
  0.6 2.0 %copy.10.cell_hbm = s32[4,8,32,8]{3,2,1,0:T(8,128)} copy(s32[4,8,32,8]{2,3,1,0:T(8,128)} %param.13) | data formatting | bytes 65536 | tf_op args[5]
  2.6 0.0 copy-done
  2.6 0.0 copy-start.1
  2.6 1.0 %copy.11.value_hbm = f32[4,8,32,8]{3,2,1,0:T(8,128)} copy(f32[4,8,32,8]{2,3,1,0:T(8,128)S(1)} %copy-done) | data formatting | bytes 65536 | tf_op args[6]
  3.6 0.0 copy-done.1
  3.6 1.0 %copy.12.weight_hbm = f32[4,8,32,8]{3,2,1,0:T(8,128)} copy(f32[4,8,32,8]{2,3,1,0:T(8,128)S(1)} %copy-done.1) | data formatting | bytes 65536 | tf_op args[7]
  4.6 38.1 %shard_map.95 = (f32[8,4,8,128]{3,2,1,0:T(8,128)}, f32[8,32,64]{2,1,0:T(8,128)}) custom-call(bf16[8,4,8,128]{3,2,1,0:T(8,128)(2,1)} %coarse_hbm.1, bf16[4,8,32,512]{3,2,1,0:T(8,128)(2,1)} %pert_hbm.1, bf16[32,32]{1,0:T(8,128)(2,1)} %lat_hbm.1, bf16[128,512]{1,0:T(8,128)(2,1)} %lon_hbm.1, f32[2,32,64]{2,1,0:T(8,128)} %wind_hbm.1, ...), custom_call_target="tpu_custom_call" | custom-call | tf_op jit(solution)/shard_map/pallas_call | solution.py:670
  42.8 0.0 copy-start.2
  42.8 1.6 %copy.15 = f32[8,4,8,128]{3,2,1,0:T(8,128)} copy(f32[8,4,8,128]{3,2,1,0:T(8,128)} %get-tuple-element.4) | data formatting | bytes 262144
  44.4 0.0 copy-done.2
  44.4 0.7 %copy.16 = f32[8,32,64]{2,1,0:T(8,128)} copy(f32[8,32,64]{2,1,0:T(8,128)S(1)} %copy-done.2) | data formatting | bytes 131072
Async XLA Ops:
  0.6 2.0 %copy-start = (f32[4,8,32,8]{2,3,1,0:T(8,128)S(1)}, f32[4,8,32,8]{2,3,1,0:T(8,128)}, u32[]{:S(2)}) copy-start(f32[4,8,32,8]{2,3,1,0:T(8,128)} %param.14) | copy-start | bytes 98308
  2.6 1.0 %copy-start.1 = (f32[4,8,32,8]{2,3,1,0:T(8,128)S(1)}, f32[4,8,32,8]{2,3,1,0:T(8,128)}, u32[]{:S(2)}) copy-start(f32[4,8,32,8]{2,3,1,0:T(8,128)} %param.15) | copy-start | bytes 98308
  42.8 1.6 %copy-start.2 = (f32[8,32,64]{2,1,0:T(8,128)S(1)}, f32[8,32,64]{2,1,0:T(8,128)}, u32[]{:S(2)}) copy-start(f32[8,32,64]{2,1,0:T(8,128)} %get-tuple-element.5) | copy-start | bytes 196612

commit v3 on v2

--- a/solution.py
+++ b/solution.py
@@ -10,6 +10,7 @@
 STEPS = 4
 OBLK = 8
 HALO = 2 * STEPS
+LAG = 3
 LANES = 128
 DIFFUSION = 0.2
 F32 = jnp.float32
@@ -63,6 +64,7 @@
     adjg,
     gb,
     gr,
+    relayed,
     in_sem,
     cg_ss,
     cg_rs,
@@ -84,6 +86,7 @@
     rel_rs,
     g_ss,
     g_rs,
+    relayed_rs,
 ):
     members, lev, rows, flon = pert_ref.shape
     clon = lon_ref.shape[0]
@@ -206,13 +209,13 @@
     for load in loads[1:-1]:
         load.wait()
 
-    blank = jnp.zeros((rows, LANES - 3 * STEPS * (cols // OBLK)), F32)
+    blank = jnp.zeros((LANES - 3 * STEPS * (cols // OBLK), rows), F32)
     winds = jnp.concatenate([wind_ref[0], wind_ref[1]], axis=1)
 
     def pack(level, carry):
         pieces = [ref[t, level] for ref in (weight_ref, value_ref) for t in range(STEPS)]
         pieces += [cell_ref[t, level].astype(F32) for t in range(STEPS)]
-        aux_ref[level, :, :LANES] = jnp.concatenate(pieces + [blank], axis=1)
+        aux_ref[level, :, :LANES] = jnp.transpose(jnp.concatenate(pieces + [blank], axis=0))
         aux_ref[level, :, LANES:] = winds
         return carry
 
@@ -532,20 +535,50 @@
     for i in range(1, npairs):
         adj_copy((pair + i) % npairs).start()
 
-    def g_copy(there, level):
-        return send(
-            gb.at[there, level], gr.at[z, level], g_ss.at[there, level], g_rs.at[z, level], me, there
-        )
-
-    def g_arrival(source, level):
-        return send(
-            gb.at[source, level],
-            gr.at[source, level],
-            g_ss.at[source, level],
-            g_rs.at[source, level],
-            me,
-            source,
-        )
+    directions = ((0, 1), (1, -1))
+
+    def g_target(way, step, k, there, level):
+        if k >= 3:
+            return z + step, relayed.at[way, there, level], relayed_rs.at[way, there, level]
+        slot = 2 * way + k - 1
+        return there, gr.at[slot, level], g_rs.at[slot, level]
+
+    def g_copy(way, step, k, level):
+        there = z + step * k
+        lat, dst, arrived = g_target(way, step, k, there, level)
+        return send(gb.at[there, level], dst, g_ss.at[there, level], arrived, me, lat)
+
+    def exists(place):
+        return (place >= 0) & (place < nlat)
+
+    def g_first(level):
+        for k in range(nlat - 1, 0, -1):
+            for way, step in directions:
+                ready = exists(z + step * k)
+                if k > 1:
+                    ready = ready & jnp.logical_not(exists(z - step))
+
+                @pl.when(ready)
+                def _():
+                    g_copy(way, step, k, level).start()
+
+    def g_later(level):
+        for k in range(nlat - 2, 1, -1):
+            for way, step in directions:
+                there = z + step * k
+
+                @pl.when(exists(there) & exists(z - step))
+                def _():
+                    send(
+                        gb.at[there, level],
+                        relayed.at[way, there, level],
+                        g_ss.at[there, level],
+                        relayed_rs.at[way, there, level],
+                        me,
+                        z - step,
+                    ).wait_recv()
+                    gb[there, level] = gb[there, level] + relayed[way, there, level]
+                    g_copy(way, step, k, level).start()
 
     def backward(level):
         field = adjg[pl.ds(level * groups, groups)].reshape(rows, flon)
@@ -561,8 +594,20 @@
         hi, lo = split2(projected)
         banded = dot(lat_t2, jnp.concatenate([hi, lo], axis=0))
         gb[:, level] = banded.reshape(nlat, -1, members * clon)
-        for i in range(1, nlat):
-            g_copy((z + i) % nlat, level).start()
+        g_first(level)
+
+    def order(j):
+        p = (pair + 2 * npairs - j) % npairs
+        if groups == 2:
+            return p
+        return 2 * p + jnp.where(j < npairs, core, 1 - core)
+
+    def step_back(j):
+        backward(order(j))
+
+        @pl.when(j >= LAG)
+        def _():
+            g_later(order(j - LAG))
 
     def near(i, carry):
         p = (pair + npairs - i) % npairs
@@ -573,7 +618,7 @@
 
         relay(p).start()
         if groups == 1:
-            backward(2 * p + core)
+            step_back(i)
         return carry
 
     lax.fori_loop(0, npairs, near, 0)
@@ -581,37 +626,46 @@
     def far(i, carry):
         p = (pair + npairs - i) % npairs
         relay_arrival(p).wait_recv()
-        if groups == 1:
-            backward(2 * p + (1 - core))
-        elif groups == 2:
-            backward(p)
-        else:
-
-            @pl.when(p % (groups // 2) == groups // 2 - 1)
-            def _():
-                backward(p // (groups // 2))
-
+        step_back(npairs + i if groups == 1 else i)
         return carry
 
     lax.fori_loop(0, npairs, far, 0)
+
+    def trail(j, carry):
+        g_later(order(j))
+        return carry
+
+    lax.fori_loop(lev - LAG, lev, trail, 0)
 
     for i in range(1, nmem):
         inc_arrival((me + nmem - i) % nmem).wait_recv()
     inc_ref[...] = incr[...]
 
-    def finish(level, carry):
-        total = gb[z, level]
-        for i in range(1, nlat):
-            source = (z + nlat - i) % nlat
-            g_arrival(source, level).wait_recv()
-            total = total + gr[source, level]
-        gb[z, level] = total
+    def finish(j, carry):
+        level = order(j)
+        for k in range(1, min(3, nlat)):
+            for way, step in directions:
+                source = z - step * k
+                slot = 2 * way + k - 1
+
+                @pl.when(exists(source))
+                def _():
+                    send(
+                        gb.at[z, level],
+                        gr.at[slot, level],
+                        g_ss.at[z, level],
+                        g_rs.at[slot, level],
+                        me,
+                        source,
+                    ).wait_recv()
+                    gb[z, level] = gb[z, level] + gr[slot, level]
+
         return carry
 
     lax.fori_loop(0, lev, finish, 0)
     for m in range(members):
         total = jnp.swapaxes(gb[z, :, :, m * clon : (m + 1) * clon], 0, 1)
-        grad_ref[:, m] = total * scale + coarse_ref[:, m].astype(F32)
+        grad_ref[:, m] = total * scale
 
     for i in range(1, nmem):
         aux_copy((me + i) % nmem).wait_send()
@@ -625,8 +679,16 @@
 
     def drain(level, carry):
         for i in range(1, nlat):
-            cg_copy((z + i) % nlat, level).wait_send()
-            g_copy((z + i) % nlat, level).wait_send()
+            there = (z + i) % nlat
+            cg_copy(there, level).wait_send()
+            send(
+                gb.at[there, level],
+                gr.at[0, level],
+                g_ss.at[there, level],
+                g_rs.at[0, level],
+                me,
+                there,
+            ).wait_send()
         return carry
 
     lax.fori_loop(0, lev, drain, 0)
@@ -652,7 +714,7 @@
     urows = rows // groups
     erows = urows + 2 * HALO
     npairs = nmem // 2
-    assert nmem == lev * groups and nmem % 2 == 0 and urows % 8 == 0 and urows >= HALO
+    assert nmem == lev * groups and nmem % 2 == 0 and groups <= 2 and urows % 8 == 0 and urows >= HALO
     assert 2 * cols == LANES and 3 * STEPS * blocks <= LANES
     vmem = pl.BlockSpec(memory_space=pltpu.VMEM)
     dma = pltpu.SemaphoreType.DMA
@@ -663,17 +725,17 @@
         lat_matrix,
         lon_matrix,
         wind_field,
-        observed_cell,
-        observed_value,
-        observed_weight,
+        jnp.swapaxes(observed_cell, 2, 3),
+        jnp.swapaxes(observed_value, 2, 3),
+        jnp.swapaxes(observed_weight, 2, 3),
     )
-    return pl.pallas_call(
+    banded, increment = pl.pallas_call(
         functools.partial(kernel, nmem, nlat, float(1.0 / (members * nmem - 1) ** 0.5)),
         out_shape=(
             jax.ShapeDtypeStruct((cband, members, lev, clon), F32),
             jax.ShapeDtypeStruct((lev, rows, cols), F32),
         ),
-        in_specs=[pl.BlockSpec(memory_space=pl.ANY)] * len(arguments),
+        in_specs=[pl.BlockSpec(memory_space=pltpu.HBM)] * len(arguments),
         out_specs=(vmem, vmem),
         scratch_shapes=[
             *[pltpu.VMEM(x.shape, x.dtype) for x in arguments],
@@ -692,7 +754,8 @@
             pltpu.VMEM((lev, rows, cols), F32),
             pltpu.VMEM((nmem, urows, flon), F32),
             pltpu.VMEM((nlat, lev, cband, width), F32),
-            pltpu.VMEM((nlat, lev, cband, width), F32),
+            pltpu.VMEM((4, lev, cband, width), F32),
+            pltpu.VMEM((2, nlat, lev, cband, width), F32),
             dma((len(arguments),)),
             dma((nlat, lev)),
             dma((nlat, lev)),
@@ -713,12 +776,14 @@
             dma((npairs,)),
             dma((npairs,)),
             dma((nlat, lev)),
-            dma((nlat, lev)),
+            dma((4, lev)),
+            dma((2, nlat, lev)),
         ],
         compiler_params=pltpu.CompilerParams(
             collective_id=0, has_side_effects=True, vmem_limit_bytes=60 * 1024 * 1024
         ),
     )(*arguments)
+    return banded + coarse_weights.astype(F32), increment
 
 
 def solution(mesh):

time: 45.2 us -> 42.7 us (0.945)
  local copies, waits for them, and re-layouts: 6.27 us -> 0.66 us
  other arithmetic: 0 us -> 1.61 us
  Pallas kernels: 38.1 us -> 39.6 us
    unnamed x11 -> x5, local copies, waits for them, and re-layouts: 6.27 us -> 0.66 us
    add x0 -> x1, other arithmetic: none -> 1.61 us  [body(): return (banded + coarse_weights.astype(F32), increment)]
    pallas_call x1, Pallas kernels: 38.1 us -> 39.6 us  [body(): pl.pallas_call(functools.partial(kernel, nmem, nlat, float(1.0 / (members...]
where the time goes in v3:
time: 42.7 us; the launch traced here: 42.5 us
  Pallas kernels  39.6 us (93%)
  other arithmetic  1.61 us (4%)
  between operations  0.67 us (2%)
  local copies, waits for them, and re-layouts  0.66 us (2%)
    pallas_call x1, Pallas kernels, body(): pl.pallas_call(functools.partial(kernel, nmem, nlat, float(1.0 / (members...  39.6 us
    add x1, other arithmetic, body(): return (banded + coarse_weights.astype(F32), increment)  1.61 us

profile of v3, /device:TPU:0, one launch (start us, length us, event | category | flops | bytes accessed | tf_op | source)
XLA Modules:
  0.0 42.5 jit_solution(5102456749753659124)
XLA Ops:
  0.6 0.0 copy-start
  0.6 39.6 %shard_map.95 = (f32[8,4,8,128]{3,2,1,0:T(8,128)}, f32[8,32,64]{2,1,0:T(8,128)}) custom-call(bf16[8,4,8,128]{3,2,1,0:T(8,128)(2,1)} %coarse_hbm.1, bf16[4,8,32,512]{3,2,1,0:T(8,128)(2,1)} %pert_hbm.1, bf16[32,32]{1,0:T(8,128)(2,1)} %lat_hbm.1, bf16[128,512]{1,0:T(8,128)(2,1)} %lon_hbm.1, f32[2,32,64]{2,1,0:T(8,128)} %wind_hbm.1, s32[4,8,8,32]{3,2,1,0:T(8,128)} %bitcast.3, ...), custom_call_target="tpu_custom_call" | custom-call | tf_op jit(solution)/shard_map/pallas_call | solution.py:732
  40.3 0.0 copy-done
  40.3 0.0 copy-start.1
  40.3 1.6 %convert_add_fusion = f32[8,4,8,128]{3,2,1,0:T(8,128)} fusion(f32[8,4,8,128]{3,2,1,0:T(8,128)} %get-tuple-element.4, bf16[8,4,8,128]{3,2,1,0:T(8,128)(2,1)S(1)} %copy-done), kind=kLoop, calls=%fused_computation | loop fusion | flops 65536 | bytes 327680 | tf_op jit(solution)/shard_map/add | solution.py:786
  41.9 0.0 copy-done.1
  41.9 0.7 %copy.11 = f32[8,32,64]{2,1,0:T(8,128)} copy(f32[8,32,64]{2,1,0:T(8,128)S(1)} %copy-done.1) | data formatting | bytes 131072
Async XLA Ops:
  0.6 39.6 %copy-start = (bf16[8,4,8,128]{3,2,1,0:T(8,128)(2,1)S(1)}, bf16[8,4,8,128]{3,2,1,0:T(8,128)(2,1)}, u32[]{:S(2)}) copy-start(bf16[8,4,8,128]{3,2,1,0:T(8,128)(2,1)} %coarse_hbm.1) | copy-start | bytes 196612
  40.3 1.6 %copy-start.1 = (f32[8,32,64]{2,1,0:T(8,128)S(1)}, f32[8,32,64]{2,1,0:T(8,128)}, u32[]{:S(2)}) copy-start(f32[8,32,64]{2,1,0:T(8,128)} %get-tuple-element.9) | copy-start | bytes 196612

commit v4 on v3

--- a/solution.py
+++ b/solution.py
@@ -65,6 +65,7 @@
     gb,
     gr,
     relayed,
+    lon_t,
     in_sem,
     cg_ss,
     cg_rs,
@@ -268,6 +269,7 @@
     lat_t = jnp.transpose(lat_f32).astype(BF16)
     lat_t2 = jnp.concatenate([lat_t, lat_t], axis=1)
     lon = lon_ref[...]
+    lon_t[...] = jnp.transpose(lon.astype(F32)).astype(BF16)
 
     loads[-1].wait()
 
@@ -294,6 +296,30 @@
             rs_copy(p).start()
 
         return carry
+
+    ah_up = send(
+        auxg.at[:, pl.ds(HALO, HALO)],
+        auxg.at[:, pl.ds(HALO + urows, HALO)],
+        ah_ss.at[0],
+        ah_rs.at[0],
+        *up,
+    )
+    ah_down = send(
+        auxg.at[:, pl.ds(urows, HALO)], auxg.at[:, pl.ds(0, HALO)], ah_ss.at[1], ah_rs.at[1], *down
+    )
+
+
+    def exchange_aux():
+        for i in range(1, nmem):
+            aux_arrival((me + nmem - i) % nmem).wait_recv()
+
+        @pl.when(has_up)
+        def _():
+            ah_up.start()
+
+        @pl.when(has_down)
+        def _():
+            ah_down.start()
 
     def forward(i, carry):
         level = level_at(i)
@@ -307,11 +333,17 @@
             [partly[:, m * clon : (m + 1) * clon] for m in range(members)], axis=0
         )
         hi, lo = split2(partly)
-        localized = dot(hi, lon) + dot(lo, lon)
+        localized = dot(jnp.concatenate([hi, lo], axis=0), lon)
+        localized = localized[: members * rows] + localized[members * rows :]
         total = localized[:rows] * pert_ref[0, level].astype(F32)
         for m in range(1, members):
             total += localized[m * rows : (m + 1) * rows] * pert_ref[m, level].astype(F32)
         part[pl.ds(level * groups, groups)] = total.reshape(groups, urows, flon)
+
+        @pl.when(i == lev // 2)
+        def _():
+            exchange_aux()
+
         if groups == 1:
 
             @pl.when(i < lev // 2)
@@ -328,27 +360,6 @@
         return carry
 
     lax.fori_loop(0, lev, forward, 0)
-
-    for i in range(1, nmem):
-        aux_arrival((me + nmem - i) % nmem).wait_recv()
-    ah_up = send(
-        auxg.at[:, pl.ds(HALO, HALO)],
-        auxg.at[:, pl.ds(HALO + urows, HALO)],
-        ah_ss.at[0],
-        ah_rs.at[0],
-        *up,
-    )
-    ah_down = send(
-        auxg.at[:, pl.ds(urows, HALO)], auxg.at[:, pl.ds(0, HALO)], ah_ss.at[1], ah_rs.at[1], *down
-    )
-
-    @pl.when(has_up)
-    def _():
-        ah_up.start()
-
-    @pl.when(has_down)
-    def _():
-        ah_down.start()
 
     if groups > 1:
         lax.fori_loop(0, npairs, combine, 0)
@@ -586,8 +597,8 @@
             [pert_ref[m, level].astype(F32) * field for m in range(members)], axis=0
         )
         hi, lo = split2(product)
-        over_lon = ((1,), (1,))
-        projected = dot(hi, lon, over_lon) + dot(lo, lon, over_lon)
+        projected = dot(jnp.concatenate([hi, lo], axis=0), lon_t[...])
+        projected = projected[: members * rows] + projected[members * rows :]
         projected = jnp.concatenate(
             [projected[m * rows : (m + 1) * rows] for m in range(members)], axis=1
         )
@@ -639,7 +650,7 @@
 
     for i in range(1, nmem):
         inc_arrival((me + nmem - i) % nmem).wait_recv()
-    inc_ref[...] = incr[...]
+    inc_ref[...] = incr[...].reshape(lev * rows, cols)
 
     def finish(j, carry):
         level = order(j)
@@ -665,7 +676,10 @@
     lax.fori_loop(0, lev, finish, 0)
     for m in range(members):
         total = jnp.swapaxes(gb[z, :, :, m * clon : (m + 1) * clon], 0, 1)
-        grad_ref[:, m] = total * scale
+        total = total * scale
+        for c in range(total.shape[0]):
+            at = (c * members + m) * lev
+            grad_ref[at : at + lev] = total[c]
 
     for i in range(1, nmem):
         aux_copy((me + i) % nmem).wait_send()
@@ -692,6 +706,11 @@
         return carry
 
     lax.fori_loop(0, lev, drain, 0)
+
+
+def finish_kernel(banded_ref, coarse_ref, tiles_ref, grad_ref, inc_ref):
+    grad_ref[...] = banded_ref[...] + coarse_ref[...].astype(F32)
+    inc_ref[...] = tiles_ref[...]
 
 
 def body(
@@ -732,8 +751,8 @@
     banded, increment = pl.pallas_call(
         functools.partial(kernel, nmem, nlat, float(1.0 / (members * nmem - 1) ** 0.5)),
         out_shape=(
-            jax.ShapeDtypeStruct((cband, members, lev, clon), F32),
-            jax.ShapeDtypeStruct((lev, rows, cols), F32),
+            jax.ShapeDtypeStruct((cband * members * lev, clon), F32),
+            jax.ShapeDtypeStruct((lev * rows, cols), F32),
         ),
         in_specs=[pl.BlockSpec(memory_space=pltpu.HBM)] * len(arguments),
         out_specs=(vmem, vmem),
@@ -756,6 +775,7 @@
             pltpu.VMEM((nlat, lev, cband, width), F32),
             pltpu.VMEM((4, lev, cband, width), F32),
             pltpu.VMEM((2, nlat, lev, cband, width), F32),
+            pltpu.VMEM((flon, clon), BF16),
             dma((len(arguments),)),
             dma((nlat, lev)),
             dma((nlat, lev)),
@@ -783,7 +803,16 @@
             collective_id=0, has_side_effects=True, vmem_limit_bytes=60 * 1024 * 1024
         ),
     )(*arguments)
-    return banded + coarse_weights.astype(F32), increment
+    gradient, increment = pl.pallas_call(
+        finish_kernel,
+        out_shape=(
+            jax.ShapeDtypeStruct((cband * members * lev, clon), F32),
+            jax.ShapeDtypeStruct((lev * rows, cols), F32),
+        ),
+        in_specs=[vmem] * 3,
+        out_specs=(vmem, vmem),
+    )(banded, coarse_weights.reshape(-1, clon), increment)
+    return gradient.reshape(coarse_weights.shape), increment.reshape(lev, rows, cols)
 
 
 def solution(mesh):

time: 42.7 us -> 41 us (0.960)
  other arithmetic: 1.61 us -> 0 us
  local copies, waits for them, and re-layouts: 0.66 us -> 0 us
  Pallas kernels: 39.6 us -> 40.2 us
    pallas_call x0 -> x1, Pallas kernels: none -> 1.72 us  [body(): pl.pallas_call(finish_kernel, out_shape=(jax.ShapeDtypeStruct((cband * me...]
    add x1 -> x0, other arithmetic: 1.61 us -> none  [body(): return (banded + coarse_weights.astype(F32), increment)]
    pallas_call x1, Pallas kernels: 39.6 us -> 38.5 us  [body(): pl.pallas_call(functools.partial(kernel, nmem, nlat, float(1.0 / (members...]
    unnamed x5 -> x0, local copies, waits for them, and re-layouts: 0.66 us -> none
where the time goes in v4:
time: 41 us; the launch traced here: 40.8 us
  Pallas kernels  40.2 us (98%)
  between operations  0.64 us (2%)
    pallas_call x1, Pallas kernels, body(): pl.pallas_call(functools.partial(kernel, nmem, nlat, float(1.0 / (members...  38.5 us
    pallas_call x1, Pallas kernels, body(): pl.pallas_call(finish_kernel, out_shape=(jax.ShapeDtypeStruct((cband * me...  1.72 us

profile of v4, /device:TPU:0, one launch (start us, length us, event | category | flops | bytes accessed | tf_op | source)
XLA Modules:
  0.0 40.8 jit_solution(18197992660065542618)
XLA Ops:
  0.6 38.5 %shard_map.95 = (f32[256,128]{1,0:T(8,128)}, f32[256,64]{1,0:T(8,128)}) custom-call(bf16[8,4,8,128]{3,2,1,0:T(8,128)(2,1)} %coarse_hbm.1, bf16[4,8,32,512]{3,2,1,0:T(8,128)(2,1)} %pert_hbm.1, bf16[32,32]{1,0:T(8,128)(2,1)} %lat_hbm.1, bf16[128,512]{1,0:T(8,128)(2,1)} %lon_hbm.1, f32[2,32,64]{2,1,0:T(8,128)} %wind_hbm.1, s32[4,8,8,32]{3,2,1,0:T(8,128)} %bitcast.7, ...), custom_call_target="tpu_custom_call" | custom-call | tf_op jit(solution)/shard_map/pallas_call | solution.py:751
  39.1 1.7 %shard_map.96 = (f32[256,128]{1,0:T(8,128)}, f32[256,64]{1,0:T(8,128)}) custom-call(f32[256,128]{1,0:T(8,128)} %get-tuple-element.6.banded_ref, bf16[256,128]{1,0:T(8,128)(2,1)} %bitcast.6, f32[256,64]{1,0:T(8,128)} %get-tuple-element.7.tiles_ref), custom_call_target="tpu_custom_call" | custom-call | tf_op jit(solution)/shard_map/pallas_call | solution.py:806

commit v5 on v4

--- a/solution.py
+++ b/solution.py
@@ -608,10 +608,11 @@
         g_first(level)
 
     def order(j):
-        p = (pair + 2 * npairs - j) % npairs
         if groups == 2:
-            return p
-        return 2 * p + jnp.where(j < npairs, core, 1 - core)
+            return (pair + npairs - j) % npairs
+        near_turn = (j == 0) | ((j >= 2) & (j <= npairs))
+        i = jnp.where(j < 2, 0, jnp.where(near_turn, j - 1, j - npairs))
+        return 2 * ((pair + npairs - i) % npairs) + jnp.where(near_turn, core, 1 - core)
 
     def step_back(j):
         backward(order(j))
@@ -629,18 +630,19 @@
 
         relay(p).start()
         if groups == 1:
-            step_back(i)
+            step_back(jnp.where(i == 0, 0, i + 1))
         return carry
 
-    lax.fori_loop(0, npairs, near, 0)
 
     def far(i, carry):
         p = (pair + npairs - i) % npairs
         relay_arrival(p).wait_recv()
-        step_back(npairs + i if groups == 1 else i)
+        step_back(jnp.where(i == 0, 1, npairs + i) if groups == 1 else i)
         return carry
 
-    lax.fori_loop(0, npairs, far, 0)
+    for first, last in ((0, 1), (1, npairs)):
+        lax.fori_loop(first, last, near, 0)
+        lax.fori_loop(first, last, far, 0)
 
     def trail(j, carry):
         g_later(order(j))

time: 41 us -> 40.4 us (0.985)
  Pallas kernels: 40.2 us -> 39.6 us
    pallas_call x1, Pallas kernels: 38.5 us -> 37.8 us  [body(): pl.pallas_call(functools.partial(kernel, nmem, nlat, float(1.0 / (members...]
where the time goes in v5:
time: 40.4 us; the launch traced here: 40.2 us
  Pallas kernels  39.6 us (98%)
  between operations  0.64 us (2%)
    pallas_call x1, Pallas kernels, body(): pl.pallas_call(functools.partial(kernel, nmem, nlat, float(1.0 / (members...  37.8 us
    pallas_call x1, Pallas kernels, body(): pl.pallas_call(finish_kernel, out_shape=(jax.ShapeDtypeStruct((cband * me...  1.72 us

profile of v5, /device:TPU:0, one launch (start us, length us, event | category | flops | bytes accessed | tf_op | source)
XLA Modules:
  0.0 40.2 jit_solution(9274481036528956249)
XLA Ops:
  0.6 37.8 %shard_map.95 = (f32[256,128]{1,0:T(8,128)}, f32[256,64]{1,0:T(8,128)}) custom-call(bf16[8,4,8,128]{3,2,1,0:T(8,128)(2,1)} %coarse_hbm.1, bf16[4,8,32,512]{3,2,1,0:T(8,128)(2,1)} %pert_hbm.1, bf16[32,32]{1,0:T(8,128)(2,1)} %lat_hbm.1, bf16[128,512]{1,0:T(8,128)(2,1)} %lon_hbm.1, f32[2,32,64]{2,1,0:T(8,128)} %wind_hbm.1, s32[4,8,8,32]{3,2,1,0:T(8,128)} %bitcast.7, ...), custom_call_target="tpu_custom_call" | custom-call | tf_op jit(solution)/shard_map/pallas_call | solution.py:753
  38.5 1.7 %shard_map.96 = (f32[256,128]{1,0:T(8,128)}, f32[256,64]{1,0:T(8,128)}) custom-call(f32[256,128]{1,0:T(8,128)} %get-tuple-element.6.banded_ref, bf16[256,128]{1,0:T(8,128)(2,1)} %bitcast.6, f32[256,64]{1,0:T(8,128)} %get-tuple-element.7.tiles_ref), custom_call_target="tpu_custom_call" | custom-call | tf_op jit(solution)/shard_map/pallas_call | solution.py:808
